TPU v7x, 256 devices: a whole 4x4x8 slice. The times are simulated.
256 devices in a mesh: date: 64 (over x_hi, y, z), strip: 4 (over x_lo, core).
Axes of the slice: x: 4 (x_hi: 2, x_lo: 2; x = x_hi * 2 + x_lo), y: 4, z: 8, core: 2. Of those that a mesh axis runs over, the one named last changes fastest.
Arguments:
- scenes: bfloat16 [2, 128, 128, 4096], P(None, 'date', 'strip'), may hold values from -6 to 6
- date_pairs: int32 [96, 2], replicated, may hold values from 0 to 127, as said below
- first_weight: bfloat16 [3, 3, 64, 2], replicated, may hold values from -4 to 4
- mid_weight: bfloat16 [2, 3, 3, 64, 64], replicated, may hold values from -0.375 to 0.375
- last_weight: bfloat16 [3, 3, 1, 64], replicated, may hold values from -0.375 to 0.375
- inversion: float32 [128, 96], replicated, may hold values from -0.625 to 0.625
Outputs:
- displacement: float32 [128, 32, 256], P('date', 'strip')
Inputs may be any that keep to these rules, and one draw needn't show every extreme that they name: `date_pairs`: Write g(d) = d // 2 for the date group of date d; in matching m, g of the reference date and g of the secondary date differ exactly in the bit of value step, and every group in 0..2 32 - 1 appears in exactly one interferogram of each matching. Which side is the reference and which date of a group is used vary.
All inputs are finite; a program needn't handle non-finite values.
Results may differ from a plain program's by a relative error of at most 0.02.
Values may be sent and summed in bfloat16 or wider, within the bound.
No kernel may reach another device: no remote copies, remote signals or barrier semaphores. Data moves between devices by JAX's collectives and lax.ppermute only.
A program may use at most 64 MiB of HBM per device.

v0:
```python
import jax
import jax.numpy as jnp
from jax import lax
from jax.sharding import PartitionSpec as P

LOOK_R = 4
LOOK_C = 16


def from_partner(block, axis, apart):
    count = lax.axis_size(axis)
    route = []
    for low in range(count):
        high = low | 1 << apart
        if high != low and high < count:
            route += [(low, high), (high, low)]
    return lax.ppermute(block, axis, route)


def extended_2(block, sides, width):
    for axis, dim in sides:
        count = lax.axis_size(axis)
        forward = [(i, i + 1) for i in range(count - 1)]
        backward = [(target, source) for source, target in forward]
        low = lax.ppermute(
            lax.slice_in_dim(block, block.shape[dim] - width, None, axis=dim), axis, forward
        )
        high = lax.ppermute(lax.slice_in_dim(block, 0, width, axis=dim), axis, backward)
        block = jnp.concatenate([low, block, high], axis=dim)
    return block


def look_sum(field):
    lead = field.shape[:-2]
    count_rows = field.shape[-2]
    count_cols = field.shape[-1]
    shaped = field.reshape(lead + (count_rows // LOOK_R, LOOK_R, count_cols // LOOK_C, LOOK_C))
    return shaped.sum(axis=(-3, -1))


def coherence_of(first, second):
    first = first.astype(jnp.float32)
    second = second.astype(jnp.float32)
    real_part = first[0] * second[0] + first[1] * second[1]
    imag_part = first[1] * second[0] - first[0] * second[1]
    first_power = first[0] * first[0] + first[1] * first[1]
    second_power = second[0] * second[0] + second[1] * second[1]
    scale = lax.rsqrt(look_sum(first_power) * look_sum(second_power) + 1e-06)
    return (jnp.stack([look_sum(real_part), look_sum(imag_part)]) * scale).astype(jnp.bfloat16)


def convolve(padded, weight):
    count_rows = padded.shape[2] - 2
    count_cols = padded.shape[3] - 2
    total = None
    for tap_row in range(3):
        for tap_col in range(3):
            piece = padded[:, :, tap_row : tap_row + count_rows, tap_col : tap_col + count_cols]
            term = jnp.einsum(
                "oi,pirc->porc", weight[tap_row, tap_col], piece, preferred_element_type=jnp.float32
            )
            total = term if total is None else total + term
    return total


def side_columns(extended, is_lower, bit_pos):
    send = jnp.where(is_lower, extended[..., -1:], extended[..., :1])
    received = from_partner(send, "date", bit_pos)
    nothing = jnp.zeros_like(received)
    left_side = jnp.where(is_lower, nothing, received)
    right_side = jnp.where(is_lower, received, nothing)
    return jnp.concatenate([left_side, extended, right_side], axis=-1)


def per_device(scenes, date_pairs, first_weight, mid_weight, last_weight, inversion):
    date_dev = scenes.shape[1]
    count_cols = scenes.shape[3]
    half_cols = count_cols // 2
    dev_count = lax.axis_size("date")
    my_index = lax.axis_index("date")
    block_size = dev_count // 2
    bit_list = [0, 1, dev_count.bit_length() - 2]
    slot_iota = jnp.arange(block_size, dtype=jnp.int32)
    lower_flags = []
    pair_index = []
    inputs = []
    for which in range(3):
        bit_pos = bit_list[which]
        block_rows = date_pairs[which * block_size : (which + 1) * block_size]
        ref_group = block_rows[:, 0] // date_dev
        sec_group = block_rows[:, 1] // date_dev
        ref_hit = ref_group == my_index
        sec_hit = sec_group == my_index
        is_ref = jnp.any(ref_hit)
        my_date = jnp.sum(
            jnp.where(ref_hit, block_rows[:, 0], 0) + jnp.where(sec_hit, block_rows[:, 1], 0)
        )
        local_date = my_date - my_index * date_dev
        pair_index.append(which * block_size + jnp.sum(jnp.where(ref_hit | sec_hit, slot_iota, 0)))
        is_lower = my_index >> bit_pos & 1 == 0
        lower_flags.append(is_lower)
        date_tile = lax.dynamic_index_in_dim(scenes, local_date, 1, keepdims=False)
        own_half = jnp.where(is_lower, date_tile[..., :half_cols], date_tile[..., half_cols:])
        send_half = jnp.where(is_lower, date_tile[..., half_cols:], date_tile[..., :half_cols])
        other_half = from_partner(send_half, "date", bit_pos)
        first = jnp.where(is_ref, own_half, other_half)
        second = jnp.where(is_ref, other_half, own_half)
        inputs.append(coherence_of(first, second))
    stacked = jnp.stack(inputs)
    weights = (
        [first_weight] + [mid_weight[inner] for inner in range(mid_weight.shape[0])] + [last_weight]
    )
    layer_count = len(weights)
    hidden = stacked
    for depth_step in range(layer_count):
        extended = extended_2(hidden, (("strip", 2),), 1)
        padded = jnp.stack(
            [
                side_columns(extended[which], lower_flags[which], bit_list[which])
                for which in range(3)
            ]
        )
        result = convolve(padded, weights[depth_step])
        if depth_step + 1 < layer_count:
            hidden = jax.nn.relu(result).astype(jnp.bfloat16)
        else:
            hidden = result.astype(jnp.bfloat16)
    phases = hidden[:, 0]
    pair_vector = jnp.stack(pair_index)
    picker = (jnp.arange(inversion.shape[1])[:, None] == pair_vector[None, :]).astype(jnp.float32)
    phase_float = phases.astype(jnp.float32)
    nothing = jnp.zeros_like(phase_float[0])
    widened = jnp.stack(
        [
            jnp.where(
                lower_flags[which],
                jnp.concatenate([phase_float[which], nothing], axis=-1),
                jnp.concatenate([nothing, phase_float[which]], axis=-1),
            )
            for which in range(3)
        ]
    )
    coef = jnp.dot(inversion, picker, precision=lax.Precision.HIGHEST)
    return lax.psum_scatter(
        jnp.einsum("dm,mrc->drc", coef, widened, precision=lax.Precision.HIGHEST),
        "date",
        scatter_dimension=0,
        tiled=True,
    )


def solution(mesh):
    return jax.shard_map(
        per_device,
        mesh=mesh,
        in_specs=(P(None, "date", "strip", None), P(), P(), P(), P(), P()),
        out_specs=P("date", "strip", None),
        check_vma=False,
    )
```

profile of v0, /device:TPU:2, one launch (start us, length us, event | category | flops | bytes accessed | tf_op | source)
XLA Modules:
  0.0 509.0 jit_solution(16482693811871125426)
XLA Ops:
  14.2 2.3 collective-permute-start.2
  19.8 3.3 collective-permute-start.1
  27.2 3.0 add.302
  49.8 2.4 collective-permute-start.3
  52.3 2.5 collective-permute-done.3
  54.9 2.3 collective-permute-start.7
  57.2 3.6 collective-permute-start.6
  67.6 1.9 collective-permute-start.9
  69.6 2.4 collective-permute-start.8
  77.7 2.1 collective-permute-start.10
  79.8 2.3 collective-permute-done.12
  82.4 2.9 collective-permute-done.11
  88.8 1.9 collective-permute-start.14
  90.7 2.4 collective-permute-start.13
  93.8 2.3 collective-permute-done.13
  96.3 2.5 collective-permute-start.17
  100.6 2.4 collective-permute-start.15
  103.5 4.0 collective-permute-done.16
  111.3 3.0 collective-permute-start.19
  114.2 1.9 collective-permute-start.18
  116.4 3.3 collective-permute-done.18
  121.1 2.4 collective-permute-start.20
  123.4 3.4 collective-permute-done.22
  134.7 367.5 %reduce-scatter.2.cloned.1.call-done = f32[2,8,256]{2,1,0:T(8,128)} async-done(((f32[128,8,256]{2,1,0:T(8,128)}), f32[2,8,256]{2,1,0:T(8,128)}) %reduce-scatter.2.cloned.1.call-update) | async-done | bytes 16400 | tf_op jit(solution)/shard_map/reduce_scatter | solution.py:144
  (176 shorter events, 63.6 us)
Async XLA Ops:
  6.5 495.7 %reduce-scatter.2.cloned.1.call-start = ((), (), s32[]{:S(2)}) async-start(), calls=%async_computation.1 | async-start | bytes 1064960 | tf_op jit(solution)/shard_map/reduce_scatter | solution.py:144
  14.2 9.6 %collective-permute-start.2 = (bf16[2,32,2048]{2,1,0:T(8,128)(2,1)S(1)}, bf16[2,32,2048]{2,1,0:T(8,128)(2,1)S(1)}, u32[]{:S(2)}, u32[]{:S(2)}) collective-permute-start(bf16[2,32,2048]{2,1,0:T(8,128)(2,1)S(1)} %broadcast_select_fusion), channel_id=1, source_target_pairs={{0,128},{128,0},{4,132},{132,4},{8,136},{136,8},{12,140},{140,12},... | collective-permute-start | bytes 786440 | tf_op jit(solution)/shard_map/ppermute | solution.py:17
  17.2 17.8 %collective-permute-start = (bf16[2,32,2048]{2,1,0:T(8,128)(2,1)}, bf16[2,32,2048]{2,1,0:T(8,128)(2,1)}, u32[]{:S(2)}, u32[]{:S(2)}) collective-permute-start(bf16[2,32,2048]{2,1,0:T(8,128)(2,1)} %broadcast_select_fusion.4), channel_id=1, source_target_pairs={{0,4},{4,0},{8,12},{12,8},{16,20},{20,16},{24,28},{28,24},{32,36},... | collective-permute-start | bytes 786440 | tf_op jit(solution)/shard_map/ppermute | solution.py:17
  19.8 22.5 %collective-permute-start.1 = (bf16[2,32,2048]{2,1,0:T(8,128)(2,1)}, bf16[2,32,2048]{2,1,0:T(8,128)(2,1)}, u32[]{:S(2)}, u32[]{:S(2)}) collective-permute-start(bf16[2,32,2048]{2,1,0:T(8,128)(2,1)} %broadcast_select_fusion.2), channel_id=1, source_target_pairs={{0,8},{8,0},{4,12},{12,4},{16,24},{24,16},{20,28},{28,20},{32,40},... | collective-permute-start | bytes 786440 | tf_op jit(solution)/shard_map/ppermute | solution.py:17
  47.9 4.3 collective-permute-start.4
  49.8 4.9 collective-permute-start.3
  54.9 7.9 %collective-permute-start.7 = (bf16[2,10,1]{2,0,1:T(2,128)(2,1)S(1)}, bf16[2,10,1]{2,0,1:T(2,128)(2,1)S(1)}, u32[]{:S(2)}, u32[]{:S(2)}) collective-permute-start(bf16[2,10,1]{2,0,1:T(2,128)(2,1)S(1)} %broadcast_select_fusion.26), channel_id=1, source_target_pairs={{0,128},{128,0},{4,132},{132,4},{8,136},{136,8},{12,140},{140,12},... | collective-permute-start | bytes 128 | tf_op jit(solution)/shard_map/ppermute | solution.py:17
  57.2 5.6 %collective-permute-start.6 = (bf16[2,10,1]{2,0,1:T(2,128)(2,1)S(1)}, bf16[2,10,1]{2,0,1:T(2,128)(2,1)S(1)}, u32[]{:S(2)}, u32[]{:S(2)}) collective-permute-start(bf16[2,10,1]{2,0,1:T(2,128)(2,1)S(1)} %broadcast_select_fusion.29), channel_id=1, source_target_pairs={{0,8},{8,0},{4,12},{12,4},{16,24},{24,16},{20,28},{28,20},{32,40},... | collective-permute-start | bytes 128 | tf_op jit(solution)/shard_map/ppermute | solution.py:17
  60.9 3.7 collective-permute-start.5
  67.6 5.7 %collective-permute-start.9 = (bf16[3,64,1,128]{3,1,2,0:T(8,128)(2,1)S(1)}, bf16[3,64,1,128]{3,1,2,0:T(8,128)(2,1)S(1)}, u32[]{:S(2)}, u32[]{:S(2)}) collective-permute-start(bf16[3,64,1,128]{3,1,2,0:T(8,128)(2,1)S(1)} %get-tuple-element.52), channel_id=1, source_target_pairs={{1,0},{2,1},{3,2},{5,4},{6,5},{7,6},{9,8},{10,9},{11,10},{13,12},{... | collective-permute-start | bytes 147464 | tf_op jit(solution)/shard_map/ppermute | solution.py:28
  69.6 5.4 %collective-permute-start.8 = (bf16[3,64,1,128]{3,1,2,0:T(8,128)(2,1)S(1)}, bf16[3,64,1,128]{3,1,2,0:T(8,128)(2,1)S(1)}, u32[]{:S(2)}, u32[]{:S(2)}) collective-permute-start(bf16[3,64,1,128]{3,1,2,0:T(8,128)(2,1)S(1)} %get-tuple-element.51), channel_id=1, source_target_pairs={{0,1},{1,2},{2,3},{4,5},{5,6},{6,7},{8,9},{9,10},{10,11},{12,13},{... | collective-permute-start | bytes 147464 | tf_op jit(solution)/shard_map/ppermute | solution.py:25
  75.2 6.9 %collective-permute-start.12 = (bf16[64,10,1]{2,0,1:T(8,128)(2,1)S(1)}, bf16[64,10,1]{2,0,1:T(8,128)(2,1)S(1)}, u32[]{:S(2)}, u32[]{:S(2)}) collective-permute-start(bf16[64,10,1]{2,0,1:T(8,128)(2,1)S(1)} %slice_select_fusion.6), channel_id=1, source_target_pairs={{0,128},{128,0},{4,132},{132,4},{8,136},{136,8},{12,140},{140,12},... | collective-permute-start | bytes 3848 | tf_op jit(solution)/shard_map/ppermute | solution.py:17
  76.7 8.6 %collective-permute-start.11 = (bf16[64,10,1]{2,0,1:T(8,128)(2,1)S(1)}, bf16[64,10,1]{2,0,1:T(8,128)(2,1)S(1)}, u32[]{:S(2)}, u32[]{:S(2)}) collective-permute-start(bf16[64,10,1]{2,0,1:T(8,128)(2,1)S(1)} %slice_select_fusion.7), channel_id=1, source_target_pairs={{0,8},{8,0},{4,12},{12,4},{16,24},{24,16},{20,28},{28,20},{32,40},... | collective-permute-start | bytes 3848 | tf_op jit(solution)/shard_map/ppermute | solution.py:17
  77.7 7.7 %collective-permute-start.10 = (bf16[64,10,1]{2,0,1:T(8,128)(2,1)S(1)}, bf16[64,10,1]{2,0,1:T(8,128)(2,1)S(1)}, u32[]{:S(2)}, u32[]{:S(2)}) collective-permute-start(bf16[64,10,1]{2,0,1:T(8,128)(2,1)S(1)} %slice_select_fusion.8), channel_id=1, source_target_pairs={{0,4},{4,0},{8,12},{12,8},{16,20},{20,16},{24,28},{28,24},{32,36},... | collective-permute-start | bytes 3848 | tf_op jit(solution)/shard_map/ppermute | solution.py:17
  88.8 5.1 collective-permute-start.14
  90.7 5.4 %collective-permute-start.13 = (bf16[3,64,1,128]{3,1,2,0:T(8,128)(2,1)S(1)}, bf16[3,64,1,128]{3,1,2,0:T(8,128)(2,1)S(1)}, u32[]{:S(2)}, u32[]{:S(2)}) collective-permute-start(bf16[3,64,1,128]{3,1,2,0:T(8,128)(2,1)S(1)} %get-tuple-element.49), channel_id=1, source_target_pairs={{0,1},{1,2},{2,3},{4,5},{5,6},{6,7},{8,9},{9,10},{10,11},{12,13},{... | collective-permute-start | bytes 147464 | tf_op jit(solution)/shard_map/ppermute | solution.py:25
  96.3 6.9 %collective-permute-start.17 = (bf16[64,10,1]{2,0,1:T(8,128)(2,1)S(1)}, bf16[64,10,1]{2,0,1:T(8,128)(2,1)S(1)}, u32[]{:S(2)}, u32[]{:S(2)}) collective-permute-start(bf16[64,10,1]{2,0,1:T(8,128)(2,1)S(1)} %slice_select_fusion.3), channel_id=1, source_target_pairs={{0,128},{128,0},{4,132},{132,4},{8,136},{136,8},{12,140},{140,12},... | collective-permute-start | bytes 3848 | tf_op jit(solution)/shard_map/ppermute | solution.py:17
  98.9 8.6 %collective-permute-start.16 = (bf16[64,10,1]{2,0,1:T(8,128)(2,1)S(1)}, bf16[64,10,1]{2,0,1:T(8,128)(2,1)S(1)}, u32[]{:S(2)}, u32[]{:S(2)}) collective-permute-start(bf16[64,10,1]{2,0,1:T(8,128)(2,1)S(1)} %slice_select_fusion.4), channel_id=1, source_target_pairs={{0,8},{8,0},{4,12},{12,4},{16,24},{24,16},{20,28},{28,20},{32,40},... | collective-permute-start | bytes 3848 | tf_op jit(solution)/shard_map/ppermute | solution.py:17
  100.6 7.4 %collective-permute-start.15 = (bf16[64,10,1]{2,0,1:T(8,128)(2,1)S(1)}, bf16[64,10,1]{2,0,1:T(8,128)(2,1)S(1)}, u32[]{:S(2)}, u32[]{:S(2)}) collective-permute-start(bf16[64,10,1]{2,0,1:T(8,128)(2,1)S(1)} %slice_select_fusion.5), channel_id=1, source_target_pairs={{0,4},{4,0},{8,12},{12,8},{16,20},{20,16},{24,28},{28,24},{32,36},... | collective-permute-start | bytes 3848 | tf_op jit(solution)/shard_map/ppermute | solution.py:17
  111.3 5.1 %collective-permute-start.19 = (bf16[3,64,1,128]{3,1,2,0:T(8,128)(2,1)S(1)}, bf16[3,64,1,128]{3,1,2,0:T(8,128)(2,1)S(1)}, u32[]{:S(2)}, u32[]{:S(2)}) collective-permute-start(bf16[3,64,1,128]{3,1,2,0:T(8,128)(2,1)S(1)} %get-tuple-element.48), channel_id=1, source_target_pairs={{1,0},{2,1},{3,2},{5,4},{6,5},{7,6},{9,8},{10,9},{11,10},{13,12},{... | collective-permute-start | bytes 147464 | tf_op jit(solution)/shard_map/ppermute | solution.py:28
  114.2 5.5 %collective-permute-start.18 = (bf16[3,64,1,128]{3,1,2,0:T(8,128)(2,1)S(1)}, bf16[3,64,1,128]{3,1,2,0:T(8,128)(2,1)S(1)}, u32[]{:S(2)}, u32[]{:S(2)}) collective-permute-start(bf16[3,64,1,128]{3,1,2,0:T(8,128)(2,1)S(1)} %get-tuple-element.47), channel_id=1, source_target_pairs={{0,1},{1,2},{2,3},{4,5},{5,6},{6,7},{8,9},{9,10},{10,11},{12,13},{... | collective-permute-start | bytes 147464 | tf_op jit(solution)/shard_map/ppermute | solution.py:25
  119.9 6.9 %collective-permute-start.22 = (bf16[64,10,1]{2,0,1:T(8,128)(2,1)S(1)}, bf16[64,10,1]{2,0,1:T(8,128)(2,1)S(1)}, u32[]{:S(2)}, u32[]{:S(2)}) collective-permute-start(bf16[64,10,1]{2,0,1:T(8,128)(2,1)S(1)} %slice_select_fusion), channel_id=1, source_target_pairs={{0,128},{128,0},{4,132},{132,4},{8,136},{136,8},{12,140},{140,12},... | collective-permute-start | bytes 3848 | tf_op jit(solution)/shard_map/ppermute | solution.py:17
  120.3 8.6 %collective-permute-start.21 = (bf16[64,10,1]{2,0,1:T(8,128)(2,1)S(1)}, bf16[64,10,1]{2,0,1:T(8,128)(2,1)S(1)}, u32[]{:S(2)}, u32[]{:S(2)}) collective-permute-start(bf16[64,10,1]{2,0,1:T(8,128)(2,1)S(1)} %slice_select_fusion.1), channel_id=1, source_target_pairs={{0,8},{8,0},{4,12},{12,4},{16,24},{24,16},{20,28},{28,20},{32,40},... | collective-permute-start | bytes 3848 | tf_op jit(solution)/shard_map/ppermute | solution.py:17
  121.1 8.1 %collective-permute-start.20 = (bf16[64,10,1]{2,0,1:T(8,128)(2,1)S(1)}, bf16[64,10,1]{2,0,1:T(8,128)(2,1)S(1)}, u32[]{:S(2)}, u32[]{:S(2)}) collective-permute-start(bf16[64,10,1]{2,0,1:T(8,128)(2,1)S(1)} %slice_select_fusion.2), channel_id=1, source_target_pairs={{0,4},{4,0},{8,12},{12,8},{16,20},{20,16},{24,28},{28,24},{32,36},... | collective-permute-start | bytes 3848 | tf_op jit(solution)/shard_map/ppermute | solution.py:17
  (4 other events, 133.6 us)
Sparse Core Ops, SparseCore 0:
  134.8 367.3 reduce-scatter.1
where the time goes:
time: 510 us; the launch traced here: 509 us
  waiting for transfers between devices  395 us (77%)
  starting transfers between devices  47 us (9%)
  other arithmetic  21.4 us (4%)
  between operations  17.6 us (3%)
  local copies, waits for them, and re-layouts  17 us (3%)
  matrix products  11.6 us (2%)
    reduce_scatter x1, waiting for transfers between devices, per_device(): lax.psum_scatter(jnp.einsum('dm,mrc->drc', coef, widened, precision=lax.P...  368 us
    ppermute x15, starting transfers between devices, from_partner(): return lax.ppermute(block, axis, route)  29.1 us
    ppermute x15, waiting for transfers between devices, from_partner(): return lax.ppermute(block, axis, route)  17.2 us
    dot_general x36, matrix products, convolve(): jnp.einsum('oi,pirc->porc', weight[tap_row, tap_col], piece, preferred_el...  10.4 us
  transfers between devices with their start and end apart: 24, of which 14 were waited for; matrix products, arithmetic and copies ran while one was open for 5% of the time, Pallas kernels for 0%

commit v1 on v0

v1 whole, which is shorter than its diff:
```python
import functools

import jax
import jax.numpy as jnp
import numpy as np
from jax import lax
from jax.experimental import pallas as pl
from jax.experimental.pallas import tpu as pltpu
from jax.sharding import PartitionSpec as P

BF = jnp.bfloat16
F32 = jnp.float32
LOOK_R = 4
LOOK_C = 16
HALO = 4
PITCH = 144
PIECE_COLS = 136
STRIP_ROWS = 8
FLAT = STRIP_ROWS * PITCH
EXT = (STRIP_ROWS + 2 * HALO) * PITCH
BITS = (0, 1, 5)
ORDER = (1, 2, 0)
SMEM = pltpu.SMEM
VMEM = pltpu.VMEM


def spec(space):
    return pl.BlockSpec(memory_space=space)


def prep_kernel(me_ref, pairs_ref, scenes_ref, send0, send1, send2, info_ref, sems):
    me = me_ref[0]
    sends = (send0, send1, send2)
    block = pairs_ref.shape[0] // 3
    width = send0.shape[2]
    total = scenes_ref.shape[3]
    copies = []
    for which in ORDER:

        def step(slot, carry):
            date, is_ref = carry
            first = pairs_ref[which * block + slot, 0]
            second = pairs_ref[which * block + slot, 1]
            hit_first = (first >> 1) == me
            hit_second = (second >> 1) == me
            date = jnp.where(hit_first, first, jnp.where(hit_second, second, date))
            return date, jnp.where(hit_first, 1, is_ref)

        date, is_ref = lax.fori_loop(0, block, step, (0, 0), unroll=True)
        local = jnp.clip(date - 2 * me, 0, 1)
        is_upper = (me >> BITS[which]) & 1
        info_ref[2 * which] = local
        info_ref[2 * which + 1] = is_ref
        start = pl.multiple_of((1 - is_upper) * (total - width), 128)
        copy = pltpu.make_async_copy(
            scenes_ref.at[:, local, :, pl.ds(start, width)], sends[which], sems.at[which]
        )
        copy.start()
        copies.append(copy)
    for copy in copies:
        copy.wait()


def coef_kernel(pairs_ref, rows_ref, coef_ref):
    block = pairs_ref.shape[0] // 3
    groups = 2 * block
    for which in range(3):

        def step(slot, carry):
            pair = which * block + slot
            first = pairs_ref[pair, 0] >> 1
            second = pairs_ref[pair, 1] >> 1
            for date in range(2):
                value = rows_ref[date, pair]
                base = (which * 2 + date) * groups
                coef_ref[base + first] = value
                coef_ref[base + second] = value
            return carry

        lax.fori_loop(0, block, step, 0, unroll=8)


def coherence_kernel(
    me_ref, info_ref, scenes_ref, recv0, recv1, recv2, out_ref, own, flat, sems
):
    me = me_ref[0]
    recvs = (recv0, recv1, recv2)
    width = recv0.shape[2]
    total = scenes_ref.shape[3]
    copies = {}
    for which in ORDER:
        is_upper = (me >> BITS[which]) & 1
        start = pl.multiple_of(is_upper * (total - width), 128)
        copies[which] = pltpu.make_async_copy(
            scenes_ref.at[:, info_ref[2 * which], :, pl.ds(start, width)],
            own.at[which],
            sems.at[which],
        )
        copies[which].start()
    lane = lax.broadcasted_iota(jnp.int32, (256, 128), 0)
    column = lax.broadcasted_iota(jnp.int32, (256, 128), 1)
    pool = jnp.where((lane & 127) >> 4 == column, 1.0, 0.0).astype(BF)
    flat[...] = jnp.zeros_like(flat)
    tiles = width // 128
    for which in ORDER:
        copies[which].wait()
        acc0 = None
        acc1 = None
        for tile in range(tiles):
            cols = slice(tile * 128, tile * 128 + 128)
            a0 = own[which, 0, :, cols].astype(F32)
            a1 = own[which, 1, :, cols].astype(F32)
            b0 = recvs[which][0, :, cols].astype(F32)
            b1 = recvs[which][1, :, cols].astype(F32)
            terms = jnp.concatenate(
                [a0 * b0 + a1 * b1, a1 * b0 - a0 * b1, a0 * a0 + a1 * a1, b0 * b0 + b1 * b1],
                axis=0,
            )
            high = terms.astype(BF)
            low = (terms - high.astype(F32)).astype(BF)
            part = jnp.dot(
                jnp.concatenate([high, low], axis=1), pool, preferred_element_type=F32
            )
            if tile == 0:
                acc0 = part
            elif tile < 16:
                acc0 = acc0 + pltpu.roll(part, 8 * tile, 1)
            else:
                acc1 = part
        sign = jnp.where(info_ref[2 * which + 1] == 1, 1.0, -1.0).astype(F32)
        for left, acc in ((0, acc0), (128, acc1)):
            grouped = acc.reshape(16, 8, 128)
            grouped = grouped + pltpu.roll(grouped, 7, 1)
            grouped = grouped + pltpu.roll(grouped, 6, 1)
            real, imag, power_a, power_b = (grouped[4 * i : 4 * i + 4] for i in range(4))
            scale = lax.rsqrt(power_a * power_b + 1e-06)
            real = real * scale
            imag = imag * (scale * sign)
            size = min(128, PITCH - left)
            for row in range(STRIP_ROWS):
                at = row * PITCH + left
                sub = 4 * (row % 2)
                for channel, value in ((0, real), (1, imag)):
                    slot = 2 * which + channel
                    flat[slot : slot + 1, at : at + size] = value[
                        row // 2, sub : sub + 1, :size
                    ]
    out_ref[...] = flat[...].astype(BF)


def conv_kernel(
    me_ref, strip_ref, own_ref, up_ref, down_ref, place_ref, w1_ref, w2_ref, w4_ref,
    out_ref, xs, taps, hidden_a, hidden_b, zs, mask_ref, phases
):
    me = me_ref[0]
    strip = strip_ref[0]
    strips = strip_ref[1]
    edge = HALO * PITCH
    row = place_ref[...] + (strip * STRIP_ROWS).astype(F32)
    limit = (strips * STRIP_ROWS).astype(F32)
    mask_ref[...] = jnp.where((row >= 0.0) & (row < limit), 1.0, 0.0).astype(F32)
    xs[:, 0:edge] = up_ref[:, FLAT - edge : FLAT].astype(F32)
    xs[:, edge : edge + FLAT] = own_ref[...].astype(F32)
    xs[:, edge + FLAT : EXT] = down_ref[:, 0:edge].astype(F32)
    x = xs[...] * mask_ref[...]
    for p in range(3):
        for q in range(3):
            shift = (p - 1) * PITCH + q - 1
            k = 3 * p + q
            moved = x if shift == 0 else pltpu.roll(x, (-shift) % EXT, 1)
            taps[8 * k : 8 * k + 8, :] = moved.astype(BF)
    hidden_a[...] = jnp.zeros_like(hidden_a)
    hidden_b[...] = jnp.zeros_like(hidden_b)

    def masked(value, lo, hi):
        rows = value.shape[0]
        value = jnp.maximum(value, 0.0).reshape(rows // 8, 8, hi - lo)
        value = value * mask_ref[:, lo:hi][None]
        return value.reshape(rows, hi - lo).astype(BF)

    def layer(source, weight, lo, hi):
        stacked = jnp.concatenate(
            [
                source[:, lo - PITCH : hi - PITCH],
                source[:, lo:hi],
                source[:, lo + PITCH : hi + PITCH],
            ],
            axis=0,
        )
        return jnp.dot(weight, stacked, preferred_element_type=F32)

    def across(parts, rows, size):
        left, mid, right = parts[0:rows], parts[rows : 2 * rows], parts[2 * rows : 3 * rows]
        return pltpu.roll(left, 1, 1) + mid + pltpu.roll(right, size - 1, 1)

    for which in range(3):
        lo, hi = 128, 2176
        value = jnp.dot(w1_ref[which], taps[:, lo:hi], preferred_element_type=F32)
        hidden_a[:, lo:hi] = masked(value, lo, hi)
        lo, hi = 256, 2048
        value = across(layer(hidden_a, w2_ref[0], lo, hi), 64, hi - lo)
        hidden_b[:, lo:hi] = masked(value, lo, hi)
        lo, hi = 384, 1920
        value = across(layer(hidden_b, w2_ref[1], lo, hi), 64, hi - lo)
        hidden_three = masked(value, lo, hi)
        value = jnp.dot(w4_ref[...], hidden_three, preferred_element_type=F32)
        zs[...] = across(value, 8, hi - lo)
        is_upper = (me >> BITS[which]) & 1
        for r in range(STRIP_ROWS):
            at = (r + HALO) * PITCH - lo
            halves = []
            for move in (0, 8):
                start = at + move
                halves.append(
                    zs[0:1, start - PITCH : start - PITCH + 128]
                    + zs[1:2, start : start + 128]
                    + zs[2:3, start + PITCH : start + PITCH + 128]
                )
            phases[r : r + 1, :] = jnp.where(is_upper == 1, halves[1], halves[0])
        phase = phases[...].astype(BF)
        for target in range(out_ref.shape[0]):
            out_ref[target, which] = phase


def sum_kernel(coef_ref, gathered_ref, out_ref):
    groups = gathered_ref.shape[0]
    acc = [[jnp.zeros((8, 128), F32) for _ in range(2)] for _ in range(2)]
    for group in range(groups):
        for which in range(3):
            side = group >> BITS[which] & 1
            phase = gathered_ref[group, which].astype(F32)
            for date in range(2):
                coef = coef_ref[(which * 2 + date) * groups + group]
                acc[date][side] = acc[date][side] + coef * phase
    for date in range(2):
        for side in range(2):
            out_ref[date, :, side * 128 : side * 128 + 128] = acc[date][side]


def place_of():
    lane = np.arange(EXT)
    row = np.where(lane % PITCH < PIECE_COLS, lane // PITCH - HALO, -1000)
    return np.broadcast_to(row.astype(np.float32), (8, EXT))


def per_device(scenes, date_pairs, first_weight, mid_weight, last_weight, inversion):
    groups = lax.axis_size("date")
    strips = lax.axis_size("strip")
    me = lax.axis_index("date").astype(jnp.int32)
    strip = lax.axis_index("strip").astype(jnp.int32)
    me_arr = me[None]
    strip_arr = jnp.stack([strip, jnp.int32(strips)])
    width = PIECE_COLS * LOOK_C
    rows = scenes.shape[2]
    ch = first_weight.shape[2]

    piece = jax.ShapeDtypeStruct((2, rows, width), BF)
    *sends, info = pl.pallas_call(
        prep_kernel,
        name="prep",
        out_shape=[piece] * 3 + [jax.ShapeDtypeStruct((8,), jnp.int32)],
        in_specs=[spec(SMEM), spec(SMEM), spec(pl.ANY)],
        out_specs=[spec(VMEM)] * 3 + [spec(SMEM)],
        scratch_shapes=[pltpu.SemaphoreType.DMA((3,))],
    )(me_arr, date_pairs, scenes)

    recvs = [None] * 3
    for which in ORDER:
        route = [(low, low ^ 1 << BITS[which]) for low in range(groups)]
        recvs[which] = lax.ppermute(sends[which], "date", route)

    own_rows = lax.dynamic_slice_in_dim(inversion, 2 * me, 2, axis=0)
    coef = pl.pallas_call(
        coef_kernel,
        name="coef",
        out_shape=jax.ShapeDtypeStruct((6 * groups,), F32),
        in_specs=[spec(SMEM), spec(SMEM)],
        out_specs=spec(SMEM),
        cost_estimate=pl.CostEstimate(flops=2000000, bytes_accessed=4000000, transcendentals=0),
    )(date_pairs, own_rows)

    looked = pl.pallas_call(
        coherence_kernel,
        name="coherence",
        out_shape=jax.ShapeDtypeStruct((8, FLAT), BF),
        in_specs=[spec(SMEM), spec(SMEM), spec(pl.ANY)] + [spec(VMEM)] * 3,
        out_specs=spec(VMEM),
        scratch_shapes=[
            pltpu.VMEM((3, 2, rows, width), BF),
            pltpu.VMEM((8, FLAT), F32),
            pltpu.SemaphoreType.DMA((3,)),
        ],
    )(me_arr, info, scenes, *recvs)

    up = lax.ppermute(looked, "strip", [(i, (i + 1) % strips) for i in range(strips)])
    down = lax.ppermute(looked, "strip", [((i + 1) % strips, i) for i in range(strips)])

    w1 = jnp.transpose(first_weight, (2, 0, 1, 3)).reshape(ch, 9, 2)
    w1 = jnp.stack(
        [jnp.pad(w1, ((0, 0), (0, 0), (2 * m, 6 - 2 * m))).reshape(ch, 72) for m in range(3)]
    )
    w2 = jnp.transpose(mid_weight, (0, 2, 3, 1, 4)).reshape(2, 3 * ch, 3 * ch)
    w4 = jnp.transpose(last_weight[:, :, 0], (1, 0, 2))
    w4 = jnp.pad(w4, ((0, 0), (0, 5), (0, 0))).reshape(24, ch)

    phases = pl.pallas_call(
        conv_kernel,
        name="convs",
        out_shape=jax.ShapeDtypeStruct((groups, 3, STRIP_ROWS, 128), BF),
        in_specs=[spec(SMEM)] * 2 + [spec(VMEM)] * 7,
        out_specs=spec(VMEM),
        scratch_shapes=[
            pltpu.VMEM((8, EXT), F32),
            pltpu.VMEM((72, EXT), BF),
            pltpu.VMEM((ch, EXT), BF),
            pltpu.VMEM((ch, EXT), BF),
            pltpu.VMEM((8, 1536), F32),
            pltpu.VMEM((8, EXT), F32),
            pltpu.VMEM((8, 128), F32),
        ],
    )(me_arr, strip_arr, looked, up, down, jnp.asarray(place_of()), w1, w2, w4)

    gathered = lax.all_to_all(phases, "date", 0, 0, tiled=True)

    return pl.pallas_call(
        sum_kernel,
        name="sums",
        out_shape=jax.ShapeDtypeStruct((2, STRIP_ROWS, 256), F32),
        in_specs=[spec(SMEM), spec(VMEM)],
        out_specs=spec(VMEM),
    )(coef, gathered)


def solution(mesh):
    return jax.shard_map(
        per_device,
        mesh=mesh,
        in_specs=(P(None, "date", "strip", None), P(), P(), P(), P(), P()),
        out_specs=P("date", "strip", None),
        check_vma=False,
    )
```

time: 510 us -> 74.5 us (0.15)
  the two profiles are of different devices: /device:TPU:2 before, /device:TPU:1 now
where the time goes in v1:
time: 74.5 us; the launch traced here: 73.9 us
  starting transfers between devices  27.1 us (36%)
  Pallas kernels  19.9 us (27%)
  waiting for transfers between devices  18.6 us (25%)
  local copies, waits for them, and re-layouts  7.06 us (9%)
  other arithmetic  1.24 us (2%)
    all_to_all x1, waiting for transfers between devices, per_device(): gathered = lax.all_to_all(phases, 'date', 0, 0, tiled=True)  13.2 us
    all_to_all x1, starting transfers between devices, per_device(): gathered = lax.all_to_all(phases, 'date', 0, 0, tiled=True)  12.5 us
    ppermute x3, starting transfers between devices, per_device(): recvs[which] = lax.ppermute(sends[which], 'date', route)  8.28 us
    pallas_call x1, Pallas kernels, per_device(): pl.pallas_call(conv_kernel, name='convs', out_shape=jax.ShapeDtypeStruct(...  7.01 us
    ppermute x1, starting transfers between devices, per_device(): lax.ppermute(looked, 'strip', [(i, (i + 1) % strips) for i in range(strip...  6.33 us
    pallas_call x1, Pallas kernels, per_device(): pl.pallas_call(coherence_kernel, name='coherence', out_shape=jax.ShapeDty...  4.63 us
    unnamed x27, local copies, waits for them, and re-layouts  4.25 us
    ppermute x3, waiting for transfers between devices, per_device(): recvs[which] = lax.ppermute(sends[which], 'date', route)  3.79 us
  transfers between devices with their start and end apart: 6, of which 4 were waited for; matrix products, arithmetic and copies ran while one was open for 5% of the time, Pallas kernels for 4%

profile of v1, /device:TPU:1, one launch (start us, length us, event | category | flops | bytes accessed | tf_op | source)
XLA Modules:
  0.0 73.9 jit_solution(9317945637291302523)
XLA Ops:
  0.0 0.7 copy-done.11
  0.7 0.7 copy.17.pairs_ref
  1.4 3.7 %prep.1 = (bf16[2,32,2176]{2,1,0:T(8,128)(2,1)}, bf16[2,32,2176]{2,1,0:T(8,128)(2,1)}, bf16[2,32,2176]{2,1,0:T(8,128)(2,1)}, s32[8]{0:T(128)}) custom-call(s32[1]{0:T(128)} %bitcast.me_ref, s32[96,2]{1,0:T(8,128)} %copy.17.pairs_ref, bf16[2,2,32,4096]{3,2,1,0:T(8,128)(2,1)} %scenes_ref.3), custom_call_target="tpu_custom_call" | custom-call | tf_op jit(solution)/shard_map/prep/pallas_call | solution.py:258
  5.1 2.5 %collective-permute-start = (bf16[2,32,2176]{2,1,0:T(8,128)(2,1)}, bf16[2,32,2176]{2,1,0:T(8,128)(2,1)S(1)}, u32[]{:S(2)}, u32[]{:S(2)}) collective-permute-start(bf16[2,32,2176]{2,1,0:T(8,128)(2,1)} %get-tuple-element.10), channel_id=1, source_target_pairs={{0,4},{4,0},{8,12},{12,8},{16,20},{20,16},{24,28},{28,24},{32,36},... | collective-permute-start | bytes 835592 | tf_op jit(solution)/shard_map/ppermute | solution.py:270
  7.6 3.0 %collective-permute-start.1 = (bf16[2,32,2176]{2,1,0:T(8,128)(2,1)}, bf16[2,32,2176]{2,1,0:T(8,128)(2,1)S(1)}, u32[]{:S(2)}, u32[]{:S(2)}) collective-permute-start(bf16[2,32,2176]{2,1,0:T(8,128)(2,1)} %get-tuple-element.11), channel_id=1, source_target_pairs={{0,8},{4,12},{8,0},{12,4},{16,24},{20,28},{24,16},{28,20},{32,40},... | collective-permute-start | bytes 835592 | tf_op jit(solution)/shard_map/ppermute | solution.py:270
  10.6 2.7 %collective-permute-start.2 = (bf16[2,32,2176]{2,1,0:T(8,128)(2,1)}, bf16[2,32,2176]{2,1,0:T(8,128)(2,1)S(1)}, u32[]{:S(2)}, u32[]{:S(2)}) collective-permute-start(bf16[2,32,2176]{2,1,0:T(8,128)(2,1)} %get-tuple-element.12), channel_id=1, source_target_pairs={{0,128},{4,132},{8,136},{12,140},{16,144},{20,148},{24,152},{28,15... | collective-permute-start | bytes 835592 | tf_op jit(solution)/shard_map/ppermute | solution.py:270
  14.3 0.6 pad_bitcast_fusion.3.w4_ref
  14.9 0.6 pad_maximum_fusion.w1_ref
  15.5 1.8 %collective-permute-done.recv0 = bf16[2,32,2176]{2,1,0:T(8,128)(2,1)S(1)} collective-permute-done((bf16[2,32,2176]{2,1,0:T(8,128)(2,1)}, bf16[2,32,2176]{2,1,0:T(8,128)(2,1)S(1)}, u32[]{:S(2)}, u32[]{:S(2)}) %collective-permute-start) | collective-permute-done | bytes 278560 | tf_op jit(solution)/shard_map/ppermute | solution.py:270
  17.3 2.0 %collective-permute-done.1.recv1 = bf16[2,32,2176]{2,1,0:T(8,128)(2,1)S(1)} collective-permute-done((bf16[2,32,2176]{2,1,0:T(8,128)(2,1)}, bf16[2,32,2176]{2,1,0:T(8,128)(2,1)S(1)}, u32[]{:S(2)}, u32[]{:S(2)}) %collective-permute-start.1) | collective-permute-done | bytes 278560 | tf_op jit(solution)/shard_map/ppermute | solution.py:270
  19.3 0.7 copy-done.4
  20.1 4.6 %coherence.1.own_ref = bf16[8,1152]{1,0:T(8,128)(2,1)} custom-call(s32[1]{0:T(128)} %bitcast.me_ref, s32[8]{0:T(128)} %get-tuple-element.9.info_ref, bf16[2,2,32,4096]{3,2,1,0:T(8,128)(2,1)} %scenes_ref.3, bf16[2,32,2176]{2,1,0:T(8,128)(2,1)} %copy-done.3, bf16[2,32,2176]{2,1,0:T(8,128)(2,1)} %copy-done.4, bf16[2,32,2176]{2,1,0:T(8,128)(2,1)} %copy-done.5), custom_call_target="tpu_custom_call" | custom-call | tf_op jit(solution)/shard_map/coherence/pallas_call | solution.py:282
  24.8 6.3 %collective-permute-start.3 = (bf16[8,1152]{1,0:T(8,128)(2,1)}, bf16[8,1152]{1,0:T(8,128)(2,1)S(1)}, u32[]{:S(2)}, u32[]{:S(2)}) collective-permute-start(bf16[8,1152]{1,0:T(8,128)(2,1)} %coherence.1.own_ref), channel_id=1, source_target_pairs={{0,1},{1,2},{2,3},{3,0},{4,5},{5,6},{6,7},{7,4},{8,9},{9,10},{10,1... | collective-permute-start | bytes 55304 | tf_op jit(solution)/shard_map/ppermute | solution.py:295
  31.1 0.6 pad_add_fusion.strip_ref
  32.0 0.9 %reshape.10.w2_ref = bf16[2,192,192]{2,1,0:T(8,128)(2,1)} reshape(bf16[2,3,64,3,64]{4,3,2,1,0:T(4,128)(2,1)S(1)} %copy.22) | data formatting | bytes 294912 | tf_op jit(solution)/shard_map/reshape | solution.py:302
  32.9 1.6 %collective-permute-done.4.down_ref = bf16[8,1152]{1,0:T(8,128)(2,1)S(1)} collective-permute-done((bf16[8,1152]{1,0:T(8,128)(2,1)}, bf16[8,1152]{1,0:T(8,128)(2,1)S(1)}, u32[]{:S(2)}, u32[]{:S(2)}) %collective-permute-start.4) | collective-permute-done | bytes 18464 | tf_op jit(solution)/shard_map/ppermute | solution.py:296
  34.5 0.6 jit_solution_.3.place_ref
  35.2 7.0 %convs.1 = bf16[64,3,8,128]{3,2,1,0:T(8,128)(2,1)} custom-call(s32[1]{0:T(128)} %bitcast.me_ref, s32[2]{0:T(128)} %pad_add_fusion.strip_ref, bf16[8,1152]{1,0:T(8,128)(2,1)} %coherence.1.own_ref, bf16[8,1152]{1,0:T(8,128)(2,1)} %copy-done.6, bf16[8,1152]{1,0:T(8,128)(2,1)} %copy-done.7, f32[8,2304]{1,0:T(8,128)} %jit_solution_.3.place_ref, ...), custom_call_target="tpu_custom_call" | custom-call | tf_op jit(solution)/shard_map/convs/pallas_call | solution.py:306
  42.2 12.5 %all-to-all-start = ((bf16[64,3,8,128]{3,2,1,0:T(8,128)(2,1)}), bf16[64,3,8,128]{3,2,1,0:T(8,128)(2,1)S(1)}, u32[]{:S(2)}, u32[]{:S(2)}) async-start(bf16[64,3,8,128]{3,2,1,0:T(8,128)(2,1)} %convs.1), calls=%async_computation | async-start | bytes 786432 | tf_op jit(solution)/shard_map/all_to_all | solution.py:323
  54.7 0.6 copy.24.rows_ref
  55.4 2.7 %coef.1.coef_ref = f32[384]{0:T(512)} custom-call(s32[96,2]{1,0:T(8,128)} %copy.17.pairs_ref, f32[2,96]{1,0:T(2,128)} %copy.24.rows_ref), custom_call_target="tpu_custom_call" | custom-call | flops 2000000 | bytes 4000000 | tf_op jit(solution)/shard_map/coef/pallas_call | solution.py:273
  58.1 13.2 %all-to-all-done.gathered_ref = bf16[64,3,8,128]{3,2,1,0:T(8,128)(2,1)S(1)} async-done(((bf16[64,3,8,128]{3,2,1,0:T(8,128)(2,1)}), bf16[64,3,8,128]{3,2,1,0:T(8,128)(2,1)S(1)}, u32[]{:S(2)}, u32[]{:S(2)}) %all-to-all-start) | async-done | bytes 393248 | tf_op jit(solution)/shard_map/all_to_all | solution.py:323
  71.3 0.8 %copy-done.1 = bf16[64,3,8,128]{3,2,1,0:T(8,128)(2,1)} copy-done((bf16[64,3,8,128]{3,2,1,0:T(8,128)(2,1)}, bf16[64,3,8,128]{3,2,1,0:T(8,128)(2,1)S(1)}, u32[]{:S(2)}) %copy-start.1) | copy-done | bytes 393240
  72.1 1.8 %sums.1 = f32[2,8,256]{2,1,0:T(8,128)} custom-call(f32[384]{0:T(512)} %coef.1.coef_ref, bf16[64,3,8,128]{3,2,1,0:T(8,128)(2,1)} %copy-done.1), custom_call_target="tpu_custom_call" | custom-call | tf_op jit(solution)/shard_map/sums/pallas_call | solution.py:325
  (31 shorter events, 1.4 us)
Async XLA Ops:
  0.0 54.6 %copy-start = (f32[128,96]{0,1:T(8,128)S(1)}, f32[128,96]{0,1:T(8,128)}, u32[]{:S(2)}) copy-start(f32[128,96]{0,1:T(8,128)} %param.12) | copy-start | bytes 147460
  0.0 0.7 copy-start.11
  5.1 8.3 %copy-start.9 = (bf16[3,3,64,2]{2,3,1,0:T(2,128)(2,1)S(1)}, bf16[3,3,64,2]{2,3,1,0:T(2,128)(2,1)}, u32[]{:S(2)}) copy-start(bf16[3,3,64,2]{2,3,1,0:T(2,128)(2,1)} %param.9) | copy-start | bytes 6916
  5.1 12.2 %collective-permute-start = (bf16[2,32,2176]{2,1,0:T(8,128)(2,1)}, bf16[2,32,2176]{2,1,0:T(8,128)(2,1)S(1)}, u32[]{:S(2)}, u32[]{:S(2)}) collective-permute-start(bf16[2,32,2176]{2,1,0:T(8,128)(2,1)} %get-tuple-element.10), channel_id=1, source_target_pairs={{0,4},{4,0},{8,12},{12,8},{16,20},{20,16},{24,28},{28,24},{32,36},... | collective-permute-start | bytes 835592 | tf_op jit(solution)/shard_map/ppermute | solution.py:270
  7.6 11.7 %collective-permute-start.1 = (bf16[2,32,2176]{2,1,0:T(8,128)(2,1)}, bf16[2,32,2176]{2,1,0:T(8,128)(2,1)S(1)}, u32[]{:S(2)}, u32[]{:S(2)}) collective-permute-start(bf16[2,32,2176]{2,1,0:T(8,128)(2,1)} %get-tuple-element.11), channel_id=1, source_target_pairs={{0,8},{4,12},{8,0},{12,4},{16,24},{20,28},{24,16},{28,20},{32,40},... | collective-permute-start | bytes 835592 | tf_op jit(solution)/shard_map/ppermute | solution.py:270
  10.6 8.7 %collective-permute-start.2 = (bf16[2,32,2176]{2,1,0:T(8,128)(2,1)}, bf16[2,32,2176]{2,1,0:T(8,128)(2,1)S(1)}, u32[]{:S(2)}, u32[]{:S(2)}) collective-permute-start(bf16[2,32,2176]{2,1,0:T(8,128)(2,1)} %get-tuple-element.12), channel_id=1, source_target_pairs={{0,128},{4,132},{8,136},{12,140},{16,144},{20,148},{24,152},{28,15... | collective-permute-start | bytes 835592 | tf_op jit(solution)/shard_map/ppermute | solution.py:270
  13.6 0.7 copy-start.10
  17.3 2.0 %copy-start.3 = (bf16[2,32,2176]{2,1,0:T(8,128)(2,1)}, bf16[2,32,2176]{2,1,0:T(8,128)(2,1)S(1)}, u32[]{:S(2)}) copy-start(bf16[2,32,2176]{2,1,0:T(8,128)(2,1)S(1)} %collective-permute-done.recv0) | copy-start | bytes 835588
  19.3 0.7 copy-start.4
  19.3 0.8 %copy-start.5 = (bf16[2,32,2176]{2,1,0:T(8,128)(2,1)}, bf16[2,32,2176]{2,1,0:T(8,128)(2,1)S(1)}, u32[]{:S(2)}) copy-start(bf16[2,32,2176]{2,1,0:T(8,128)(2,1)S(1)} %collective-permute-done.2.recv2) | copy-start | bytes 835588
  20.1 11.6 %copy-start.2 = (bf16[2,3,3,64,64]{4,3,2,1,0:T(8,128)(2,1)S(1)}, bf16[2,3,3,64,64]{4,3,2,1,0:T(8,128)(2,1)}, u32[]{:S(2)}) copy-start(bf16[2,3,3,64,64]{4,3,2,1,0:T(8,128)(2,1)} %param.10) | copy-start | bytes 442372
  24.8 8.2 %collective-permute-start.3 = (bf16[8,1152]{1,0:T(8,128)(2,1)}, bf16[8,1152]{1,0:T(8,128)(2,1)S(1)}, u32[]{:S(2)}, u32[]{:S(2)}) collective-permute-start(bf16[8,1152]{1,0:T(8,128)(2,1)} %coherence.1.own_ref), channel_id=1, source_target_pairs={{0,1},{1,2},{2,3},{3,0},{4,5},{5,6},{6,7},{7,4},{8,9},{9,10},{10,1... | collective-permute-start | bytes 55304 | tf_op jit(solution)/shard_map/ppermute | solution.py:295
  31.1 3.4 %collective-permute-start.4 = (bf16[8,1152]{1,0:T(8,128)(2,1)}, bf16[8,1152]{1,0:T(8,128)(2,1)S(1)}, u32[]{:S(2)}, u32[]{:S(2)}) collective-permute-start(bf16[8,1152]{1,0:T(8,128)(2,1)} %coherence.1.own_ref), channel_id=1, source_target_pairs={{1,0},{2,1},{3,2},{0,3},{5,4},{6,5},{7,6},{4,7},{9,8},{10,9},{11,1... | collective-permute-start | bytes 55304 | tf_op jit(solution)/shard_map/ppermute | solution.py:296
  32.0 2.5 %copy-start.8 = (f32[2304]{0:T(1024)S(1)}, f32[2304]{0:T(1024)}, u32[]{:S(2)}) copy-start(f32[2304]{0:T(1024)} %constant.21.clone) | copy-start | bytes 27652
  32.9 2.2 %copy-start.6 = (bf16[8,1152]{1,0:T(8,128)(2,1)}, bf16[8,1152]{1,0:T(8,128)(2,1)S(1)}, u32[]{:S(2)}) copy-start(bf16[8,1152]{1,0:T(8,128)(2,1)S(1)} %collective-permute-done.3.up_ref) | copy-start | bytes 55300
  34.5 0.6 copy-start.7
  42.2 29.2 %all-to-all-start = ((bf16[64,3,8,128]{3,2,1,0:T(8,128)(2,1)}), bf16[64,3,8,128]{3,2,1,0:T(8,128)(2,1)S(1)}, u32[]{:S(2)}, u32[]{:S(2)}) async-start(bf16[64,3,8,128]{3,2,1,0:T(8,128)(2,1)} %convs.1), calls=%async_computation | async-start | bytes 786432 | tf_op jit(solution)/shard_map/all_to_all | solution.py:323
  71.3 0.8 %copy-start.1 = (bf16[64,3,8,128]{3,2,1,0:T(8,128)(2,1)}, bf16[64,3,8,128]{3,2,1,0:T(8,128)(2,1)S(1)}, u32[]{:S(2)}) copy-start(bf16[64,3,8,128]{3,2,1,0:T(8,128)(2,1)S(1)} %all-to-all-done.gathered_ref) | copy-start | bytes 1179652

commit v2 on v1

v2 whole, which is shorter than its diff:
```python
import functools

import jax
import jax.numpy as jnp
from jax import lax
from jax.experimental import pallas as pl
from jax.experimental.pallas import tpu as pltpu
from jax.sharding import PartitionSpec as P


BF = jnp.bfloat16
F32 = jnp.float32
LOOK_C = 16
HALO = 4
PITCH = 144
PIECE_COLS = 136
STRIP_ROWS = 8
FLAT = STRIP_ROWS * PITCH
EXT = (STRIP_ROWS + 2 * HALO) * PITCH
BITS = (0, 1, 5)
SWAPS = (2, 1, 0)
GROUPS = ((2,), (0,), (1,))
PART = 8 * PITCH
SMEM = pltpu.SMEM
VMEM = pltpu.VMEM


def in_vmem(x):
    return pltpu.with_memory_space_constraint(x, pltpu.VMEM)


def spec(space):
    return pl.BlockSpec(memory_space=space)


def prep_kernel(pairs_ref, scenes_ref, *refs):
    *sends, info_ref, sems = refs
    me = lax.axis_index("date")
    both = pairs_ref[...]
    block = both.shape[1] // 3
    lane = lax.broadcasted_iota(jnp.int32, both.shape, 1)
    side = lax.broadcasted_iota(jnp.int32, both.shape, 0)
    code = (both & 1) + jnp.where(side == 0, 2, 0)
    weight = jnp.where(lane < block, 1, jnp.where(lane < 2 * block, 4, 16))
    code = jnp.where((both >> 1) == me, code * weight, 0).astype(F32)
    packed = jnp.sum(code).astype(jnp.int32)
    width = sends[0].shape[2]
    total = scenes_ref.shape[3]
    copies = []
    for slot, which in enumerate(SWAPS):
        local = (packed >> (2 * which)) & 1
        is_upper = (me >> BITS[which]) & 1
        start = pl.multiple_of((1 - is_upper) * (total - width), 128)
        copy = pltpu.make_async_copy(
            scenes_ref.at[:, local, :, pl.ds(start, width)], sends[slot], sems.at[slot]
        )
        copy.start()
        copies.append(copy)
        info_ref[2 * which] = local
        info_ref[2 * which + 1] = (packed >> (2 * which + 1)) & 1
    for copy in copies:
        copy.wait()


def own_kernel(info_ref, scenes_ref, *refs):
    *owns, sign_ref, sems = refs
    me = lax.axis_index("date")
    width = owns[0].shape[2]
    total = scenes_ref.shape[3]
    copies = []
    for which, own in enumerate(owns):
        is_upper = (me >> BITS[which]) & 1
        start = pl.multiple_of(is_upper * (total - width), 128)
        copy = pltpu.make_async_copy(
            scenes_ref.at[:, info_ref[2 * which], :, pl.ds(start, width)], own, sems.at[which]
        )
        copy.start()
        copies.append(copy)
        sign = jnp.where(info_ref[2 * which + 1] == 1, 1.0, -1.0).astype(F32)
        sign_ref[which] = jnp.full(sign_ref.shape[1:], sign, F32)
    for copy in copies:
        copy.wait()


def coef_kernel(pairs_ref, rows_ref, coef_ref):
    block = pairs_ref.shape[1] // 3
    groups = 2 * block
    for which in range(3):

        def step(slot, carry):
            pair = which * block + slot
            first = pairs_ref[0, pair] >> 1
            second = pairs_ref[1, pair] >> 1
            for date in range(2):
                value = rows_ref[date, pair]
                base = (which * 2 + date) * groups
                coef_ref[base + first] = value
                coef_ref[base + second] = value
            return carry

        lax.fori_loop(0, block, step, 0, unroll=8)


def coherence_kernel(matchings, sign_ref, *refs):
    count = len(matchings)
    recvs = refs[:count]
    owns = refs[count : 2 * count]
    out_ref, flat = refs[2 * count :]
    width = recvs[0].shape[2]
    lane = lax.broadcasted_iota(jnp.int32, (256, 128), 0)
    column = lax.broadcasted_iota(jnp.int32, (256, 128), 1)
    pool = jnp.where((lane & 127) >> 4 == column, 1.0, 0.0).astype(BF)
    flat[...] = jnp.zeros_like(flat)
    tiles = width // 128
    for slot, which in enumerate(matchings):
        acc0 = None
        acc1 = None
        for tile in range(tiles):
            cols = slice(tile * 128, tile * 128 + 128)
            a0 = owns[slot][0, :, cols].astype(F32)
            a1 = owns[slot][1, :, cols].astype(F32)
            b0 = recvs[slot][0, :, cols].astype(F32)
            b1 = recvs[slot][1, :, cols].astype(F32)
            terms = jnp.concatenate(
                [a0 * b0 + a1 * b1, a1 * b0 - a0 * b1, a0 * a0 + a1 * a1, b0 * b0 + b1 * b1],
                axis=0,
            )
            high = terms.astype(BF)
            low = (terms - high.astype(F32)).astype(BF)
            part = jnp.dot(
                jnp.concatenate([high, low], axis=1), pool, preferred_element_type=F32
            )
            if tile == 0:
                acc0 = part
            elif tile < 16:
                acc0 = acc0 + pltpu.roll(part, 8 * tile, 1)
            else:
                acc1 = part
        sign = sign_ref[which][None]
        for left, acc in ((0, acc0), (128, acc1)):
            grouped = acc.reshape(16, 8, 128)
            grouped = grouped + pltpu.roll(grouped, 7, 1)
            grouped = grouped + pltpu.roll(grouped, 6, 1)
            real, imag, power_a, power_b = (grouped[4 * i : 4 * i + 4] for i in range(4))
            scale = lax.rsqrt(power_a * power_b + 1e-06)
            real = real * scale
            imag = imag * (scale * sign)
            size = min(128, PITCH - left)
            for row in range(STRIP_ROWS):
                at = (row % 2) * (FLAT // 2) + (row // 2) * PITCH + left
                sub = 4 * (row % 2)
                for channel, value in ((0, real), (1, imag)):
                    line = 2 * slot + channel
                    flat[line : line + 1, at : at + size] = value[
                        row // 2, sub : sub + 1, :size
                    ]
    out_ref[...] = flat[...].astype(BF)


def conv_kernel(
    matchings, own_ref, up_ref, down_ref, w1_ref, w2_ref, w4_ref, *refs
):
    out_ref, xs, taps, hidden_a, hidden_b, zs, mask_ref, phases = refs[-8:]
    others = refs[:-8]
    me = lax.axis_index("date")
    strip = lax.axis_index("strip")
    strips = lax.axis_size("strip")
    guard = 128
    lane = lax.broadcasted_iota(jnp.int32, (8, 2 * PART), 1).astype(F32)
    odd = jnp.where(lane >= PART, 1.0, 0.0).astype(F32)
    lane = lane - PART * odd
    row = jnp.floor((lane + 0.5) * (1.0 / PITCH))
    column = lane - row * PITCH
    row = 2.0 * row + odd + (strip * STRIP_ROWS - HALO).astype(F32)
    limit = float(strips * STRIP_ROWS)
    mask_ref[...] = jnp.where(
        (row >= 0.0) & (row < limit) & (column < PIECE_COLS), 1.0, 0.0
    ).astype(F32)
    edge = HALO // 2 * PITCH
    for part in range(2):
        base = part * PART
        half = part * (FLAT // 2)
        xs[:, base : base + edge] = up_ref[:, half + edge : half + 2 * edge].astype(F32)
        xs[:, base + edge : base + 3 * edge] = own_ref[:, half : half + 2 * edge].astype(F32)
        xs[:, base + 3 * edge : base + PART] = down_ref[:, half : half + edge].astype(F32)
    even = xs[:, :PART] * mask_ref[:, :PART]
    odd = xs[:, PART:] * mask_ref[:, PART:]
    sources = (
        (pltpu.roll(odd, PITCH, 1), even),
        (even, odd),
        (odd, pltpu.roll(even, PART - PITCH, 1)),
    )
    for p in range(3):
        for part in range(2):
            base = part * PART
            for q in range(3):
                k = 8 * (3 * p + q)
                value = sources[p][part]
                if q != 1:
                    value = pltpu.roll(value, 1 if q == 0 else PART - 1, 1)
                taps[k : k + 8, base : base + PART] = value.astype(BF)
    hidden_a[...] = jnp.zeros_like(hidden_a)
    hidden_b[...] = jnp.zeros_like(hidden_b)

    def masked(value, part, lo, hi):
        lo, hi = part * PART + lo, part * PART + hi
        rows = value.shape[0]
        value = jnp.maximum(value, 0.0).reshape(rows // 8, 8, hi - lo)
        value = value * mask_ref[:, lo:hi][None]
        return value.reshape(rows, hi - lo).astype(BF)

    def terms(hidden, weight, part, lo, hi):
        stacked = jnp.concatenate(
            [hidden[part, :, guard + lo + q - 1 : guard + hi + q - 1] for q in range(3)],
            axis=0,
        )
        value = jnp.dot(weight, stacked, preferred_element_type=F32)
        rows = value.shape[0] // 3
        return [value[p * rows : p * rows + rows] for p in range(3)]

    def joined(hidden, weight, ranges, outs):
        (e_lo, e_hi), (o_lo, o_hi) = ranges
        from_even = terms(hidden, weight, 0, e_lo, e_hi)
        from_odd = terms(hidden, weight, 1, o_lo, o_hi)
        lo, hi = outs[0]
        to_even = (
            from_even[1][:, lo - e_lo : hi - e_lo]
            + from_odd[2][:, lo - o_lo : hi - o_lo]
            + pltpu.roll(from_odd[0], PITCH, 1)[:, lo - o_lo : hi - o_lo]
        )
        lo, hi = outs[1]
        to_odd = (
            from_odd[1][:, lo - o_lo : hi - o_lo]
            + from_even[0][:, lo - e_lo : hi - e_lo]
            + pltpu.roll(from_even[2], e_hi - e_lo - PITCH, 1)[:, lo - e_lo : hi - e_lo]
        )
        return to_even, to_odd

    for slot, which in enumerate(matchings):
        for part, (lo, hi) in enumerate(((128, 1152), (0, 1024))):
            base = part * PART
            value = jnp.dot(
                w1_ref[slot], taps[:, base + lo : base + hi], preferred_element_type=F32
            )
            hidden_a[part, :, guard + lo : guard + hi] = masked(value, part, lo, hi)
        outs = ((128, 1024), (128, 1024))
        both = joined(hidden_a, w2_ref[0], ((128, 1152), (0, 1024)), outs)
        for part, (lo, hi) in enumerate(outs):
            hidden_b[part, :, guard + lo : guard + hi] = masked(both[part], part, lo, hi)
        outs = ((256, 1024), (128, 896))
        both = joined(hidden_b, w2_ref[1], ((128, 1024), (128, 1024)), outs)
        is_upper = (me >> BITS[which]) & 1
        for part, (lo, hi) in enumerate(outs):
            value = masked(both[part], part, lo, hi)
            value = jnp.dot(w4_ref[...], value, preferred_element_type=F32)
            value = (
                pltpu.roll(value[0:8], 1, 1)
                + value[8:16]
                + pltpu.roll(value[16:24], hi - lo - 1, 1)
            )
            zs[part] = jnp.where(is_upper == 1, pltpu.roll(value, hi - lo - 8, 1), value)
        for r in range(STRIP_ROWS):
            at = (r // 2 + HALO // 2) * PITCH
            if r % 2 == 0:
                picks = ((0, 1, 0), (1, 2, 0), (1, 0, -PITCH))
            else:
                picks = ((1, 1, 0), (0, 0, 0), (0, 2, PITCH))
            total = None
            for part, p, move in picks:
                start = at + move - outs[part][0]
                value = zs[part, p : p + 1, start : start + 128]
                total = value if total is None else total + value
            phases[r : r + 1, :] = total
        phase = phases[...].astype(BF)
        if len(out_ref.shape) == 3:
            out_ref[slot] = phase
        else:
            for target in range(out_ref.shape[0]):
                out_ref[target, which] = phase
    if len(out_ref.shape) == 4:
        rest = [which for which in range(3) if which not in matchings]
        for which, phase_ref in zip(rest, others):
            phase = phase_ref[0]
            for target in range(out_ref.shape[0]):
                out_ref[target, which] = phase


def sum_kernel(coef_ref, gathered_ref, out_ref):
    groups = gathered_ref.shape[0]
    acc = [[jnp.zeros((8, 128), F32) for _ in range(2)] for _ in range(2)]
    for group in range(groups):
        for which in range(3):
            side = group >> BITS[which] & 1
            phase = gathered_ref[group, which].astype(F32)
            for date in range(2):
                coef = coef_ref[(which * 2 + date) * groups + group]
                acc[date][side] = acc[date][side] + coef * phase
    for date in range(2):
        for side in range(2):
            out_ref[date, :, side * 128 : side * 128 + 128] = acc[date][side]


def per_device(scenes, date_pairs, first_weight, mid_weight, last_weight, inversion):
    groups = lax.axis_size("date")
    strips = lax.axis_size("strip")
    me = lax.axis_index("date").astype(jnp.int32)
    width = PIECE_COLS * LOOK_C
    rows = scenes.shape[2]
    ch = first_weight.shape[2]
    pairs = date_pairs.T

    piece = (2, rows, width)
    *sends, info = pl.pallas_call(
        prep_kernel,
        name="prep",
        out_shape=[pltpu.VMEM(piece, BF)] * 3 + [jax.ShapeDtypeStruct((8,), jnp.int32)],
        in_specs=[spec(VMEM), spec(pl.ANY)],
        out_specs=[spec(VMEM)] * 3 + [spec(SMEM)],
        scratch_shapes=[pltpu.SemaphoreType.DMA((3,))],
    )(pairs, scenes)
    *owns, signs = pl.pallas_call(
        own_kernel,
        name="own",
        out_shape=[pltpu.VMEM(piece, BF)] * 3 + [pltpu.VMEM((3, 8, 128), F32)],
        in_specs=[spec(SMEM), spec(pl.ANY)],
        out_specs=[spec(VMEM)] * 4,
        scratch_shapes=[pltpu.SemaphoreType.DMA((3,))],
    )(info, scenes)

    recvs = {}
    for slot, which in enumerate(SWAPS):
        route = [(low, low ^ 1 << BITS[which]) for low in range(groups)]
        recvs[which] = lax.ppermute(sends[slot], "date", route)

    own_rows = lax.dynamic_slice_in_dim(inversion, 2 * me, 2, axis=0)
    coef = pl.pallas_call(
        coef_kernel,
        name="coef",
        out_shape=jax.ShapeDtypeStruct((6 * groups,), F32),
        in_specs=[spec(SMEM), spec(SMEM)],
        out_specs=spec(SMEM),
        cost_estimate=pl.CostEstimate(flops=2000000, bytes_accessed=4000000, transcendentals=0),
    )(pairs, own_rows)

    w1 = jnp.transpose(first_weight, (2, 0, 1, 3)).reshape(ch, 9, 2)
    w1 = jnp.stack(
        [jnp.pad(w1, ((0, 0), (0, 0), (2 * m, 6 - 2 * m))).reshape(ch, 72) for m in range(2)]
    )
    w2 = jnp.transpose(mid_weight, (0, 1, 3, 2, 4)).reshape(2, 3 * ch, 3 * ch)
    w4 = jnp.transpose(last_weight[:, :, 0], (1, 0, 2))
    w4 = jnp.pad(w4, ((0, 0), (0, 5), (0, 0))).reshape(24, ch)

    def looked_of(matchings):
        count = len(matchings)
        looked = pl.pallas_call(
            functools.partial(coherence_kernel, matchings),
            out_shape=pltpu.VMEM((8, FLAT), BF),
            in_specs=[spec(VMEM)] * (1 + 2 * count),
            out_specs=spec(VMEM),
            scratch_shapes=[pltpu.VMEM((8, FLAT), F32)],
        )(
            in_vmem(signs),
            *[in_vmem(recvs[which]) for which in matchings],
            *[in_vmem(owns[which]) for which in matchings],
        )
        up = lax.ppermute(looked, "strip", [(i, (i + 1) % strips) for i in range(strips)])
        down = lax.ppermute(looked, "strip", [((i + 1) % strips, i) for i in range(strips)])
        return looked, up, down

    def phases_of(matchings, looked, shape, *more):
        return pl.pallas_call(
            functools.partial(conv_kernel, matchings),
            out_shape=pltpu.VMEM(shape, BF),
            in_specs=[spec(VMEM)] * (6 + len(more)),
            out_specs=spec(VMEM),
            scratch_shapes=[
                pltpu.VMEM((8, EXT), F32),
                pltpu.VMEM((72, EXT), BF),
                pltpu.VMEM((2, ch, PART + 256), BF),
                pltpu.VMEM((2, ch, PART + 256), BF),
                pltpu.VMEM((2, 8, 768), F32),
                pltpu.VMEM((8, EXT), F32),
                pltpu.VMEM((8, 128), F32),
            ],
        )(
            *[in_vmem(v) for v in looked], *[in_vmem(v) for v in (w1, w2, w4)],
            *[in_vmem(v) for v in more],
        )

    done = []
    looked = [looked_of(group) for group in GROUPS]
    for group, value in zip(GROUPS, looked):
        if group is not GROUPS[-1]:
            shape = (len(group), STRIP_ROWS, 128)
            done.append(phases_of(group, value, shape))
    by_matching = {group[0]: value for group, value in zip(GROUPS, done)}
    rest = [by_matching[which] for which in sorted(by_matching)]
    shape = (groups, 3, STRIP_ROWS, 128)
    phases = phases_of(GROUPS[-1], looked[-1], shape, *rest)

    gathered = lax.all_to_all(phases, "date", 0, 0, tiled=True)

    return pl.pallas_call(
        sum_kernel,
        name="sums",
        out_shape=jax.ShapeDtypeStruct((2, STRIP_ROWS, 256), F32),
        in_specs=[spec(SMEM), spec(VMEM)],
        out_specs=spec(VMEM),
    )(coef, in_vmem(gathered))


def solution(mesh):
    return jax.shard_map(
        per_device,
        mesh=mesh,
        in_specs=(P(None, "date", "strip", None), P(), P(), P(), P(), P()),
        out_specs=P("date", "strip", None),
        check_vma=False,
    )
```

time: 74.5 us -> 65.7 us (0.88)
  the two profiles are of different devices: /device:TPU:1 before, /device:TPU:2 now
where the time goes in v2:
time: 65.7 us; the launch traced here: 64.5 us
  starting transfers between devices  22.9 us (35%)
  waiting for transfers between devices  21.9 us (33%)
  Pallas kernels  17.4 us (26%)
  local copies, waits for them, and re-layouts  2.11 us (3%)
    all_to_all x1, waiting for transfers between devices, per_device(): gathered = lax.all_to_all(phases, 'date', 0, 0, tiled=True)  15.6 us
    all_to_all x1, starting transfers between devices, per_device(): gathered = lax.all_to_all(phases, 'date', 0, 0, tiled=True)  12.9 us
    ppermute x3, starting transfers between devices, per_device(): recvs[which] = lax.ppermute(sends[slot], 'date', route)  7.42 us
    pallas_call x3, Pallas kernels, phases_of(): pl.pallas_call(functools.partial(conv_kernel, matchings), out_shape=pltpu...  7.42 us
    ppermute x3, waiting for transfers between devices, per_device(): recvs[which] = lax.ppermute(sends[slot], 'date', route)  5.89 us
    pallas_call x1, Pallas kernels, per_device(): pl.pallas_call(prep_kernel, name='prep', out_shape=[pltpu.VMEM(piece, BF)...  2.54 us
    pallas_call x1, Pallas kernels, per_device(): pl.pallas_call(own_kernel, name='own', out_shape=[pltpu.VMEM(piece, BF)]...  2.16 us
    pallas_call x3, Pallas kernels, looked_of(): pl.pallas_call(functools.partial(coherence_kernel, matchings), out_shape=...  1.9 us
  transfers between devices with their start and end apart: 10, of which 4 were waited for; matrix products, arithmetic and copies ran while one was open for 2% of the time, Pallas kernels for 16%

profile of v2, /device:TPU:2, one launch (start us, length us, event | category | flops | bytes accessed | tf_op | source)
XLA Modules:
  0.0 64.5 jit_solution(10852733248053120548)
XLA Ops:
  0.0 2.5 %prep.1 = (bf16[2,32,2176]{2,1,0:T(8,128)(2,1)S(1)}, bf16[2,32,2176]{2,1,0:T(8,128)(2,1)S(1)}, bf16[2,32,2176]{2,1,0:T(8,128)(2,1)S(1)}, s32[8]{0:T(128)}) custom-call(s32[2,96]{1,0:T(2,128)} %bitcast.17, bf16[2,2,32,4096]{3,2,1,0:T(8,128)(2,1)} %scenes_ref.3), custom_call_target="tpu_custom_call" | custom-call | tf_op jit(solution)/shard_map/prep/pallas_call | solution.py:313
  2.6 1.9 %collective-permute-start.3 = (bf16[2,32,2176]{2,1,0:T(8,128)(2,1)S(1)}, bf16[2,32,2176]{2,1,0:T(8,128)(2,1)S(1)}, u32[]{:S(2)}, u32[]{:S(2)}) collective-permute-start(bf16[2,32,2176]{2,1,0:T(8,128)(2,1)S(1)} %get-tuple-element.17), channel_id=1, source_target_pairs={{0,4},{4,0},{8,12},{12,8},{16,20},{20,16},{24,28},{28,24},{32,36},... | collective-permute-start | bytes 835592 | tf_op jit(solution)/shard_map/ppermute | solution.py:333
  4.5 3.3 %collective-permute-start = (bf16[2,32,2176]{2,1,0:T(8,128)(2,1)S(1)}, bf16[2,32,2176]{2,1,0:T(8,128)(2,1)S(1)}, u32[]{:S(2)}, u32[]{:S(2)}) collective-permute-start(bf16[2,32,2176]{2,1,0:T(8,128)(2,1)S(1)} %get-tuple-element.15), channel_id=1, source_target_pairs={{0,8},{4,12},{8,0},{12,4},{16,24},{20,28},{24,16},{28,20},{32,40},... | collective-permute-start | bytes 835592 | tf_op jit(solution)/shard_map/ppermute | solution.py:333
  7.8 2.2 %collective-permute-start.6 = (bf16[2,32,2176]{2,1,0:T(8,128)(2,1)S(1)}, bf16[2,32,2176]{2,1,0:T(8,128)(2,1)S(1)}, u32[]{:S(2)}, u32[]{:S(2)}) collective-permute-start(bf16[2,32,2176]{2,1,0:T(8,128)(2,1)S(1)} %get-tuple-element.19), channel_id=1, source_target_pairs={{0,128},{4,132},{8,136},{12,140},{16,144},{20,148},{24,152},{28,15... | collective-permute-start | bytes 835592 | tf_op jit(solution)/shard_map/ppermute | solution.py:333
  10.2 2.2 %own.1 = (bf16[2,32,2176]{2,1,0:T(8,128)(2,1)S(1)}, bf16[2,32,2176]{2,1,0:T(8,128)(2,1)S(1)}, bf16[2,32,2176]{2,1,0:T(8,128)(2,1)S(1)}, f32[3,8,128]{2,1,0:T(8,128)S(1)}) custom-call(s32[8]{0:T(128)} %get-tuple-element.13.info_ref, bf16[2,2,32,4096]{3,2,1,0:T(8,128)(2,1)} %scenes_ref.3), custom_call_target="tpu_custom_call" | custom-call | tf_op jit(solution)/shard_map/own/pallas_call | solution.py:321
  12.4 4.5 %collective-permute-done.3.refs_0_ = bf16[2,32,2176]{2,1,0:T(8,128)(2,1)S(1)} collective-permute-done((bf16[2,32,2176]{2,1,0:T(8,128)(2,1)S(1)}, bf16[2,32,2176]{2,1,0:T(8,128)(2,1)S(1)}, u32[]{:S(2)}, u32[]{:S(2)}) %collective-permute-start.3) | collective-permute-done | bytes 278560 | tf_op jit(solution)/shard_map/ppermute | solution.py:333
  16.9 0.6 shard_map.65.own_ref
  17.7 0.7 %copy-done.3 = bf16[3,3,1,64]{3,1,2,0:T(4,128)(2,1)S(1)} copy-done((bf16[3,3,1,64]{3,1,2,0:T(4,128)(2,1)S(1)}, bf16[3,3,1,64]{3,1,2,0:T(4,128)(2,1)}, u32[]{:S(2)}) %copy-start.3) | copy-done | bytes 1176
  18.3 0.5 collective-permute-start.4
  18.8 1.3 %collective-permute-done.refs_0_ = bf16[2,32,2176]{2,1,0:T(8,128)(2,1)S(1)} collective-permute-done((bf16[2,32,2176]{2,1,0:T(8,128)(2,1)S(1)}, bf16[2,32,2176]{2,1,0:T(8,128)(2,1)S(1)}, u32[]{:S(2)}, u32[]{:S(2)}) %collective-permute-start) | collective-permute-done | bytes 278560 | tf_op jit(solution)/shard_map/ppermute | solution.py:333
  20.2 0.6 shard_map.64.own_ref
  20.9 0.5 collective-permute-start.1
  21.4 0.6 shard_map.67.own_ref
  22.0 1.4 %collective-permute-start.8 = (bf16[8,1152]{1,0:T(8,128)(2,1)S(1)}, bf16[8,1152]{1,0:T(8,128)(2,1)S(1)}, u32[]{:S(2)}, u32[]{:S(2)}) collective-permute-start(bf16[8,1152]{1,0:T(8,128)(2,1)S(1)} %shard_map.67.own_ref), channel_id=1, source_target_pairs={{1,0},{2,1},{3,2},{0,3},{5,4},{6,5},{7,6},{4,7},{9,8},{10,9},{11,1... | collective-permute-start | bytes 55304 | tf_op jit(solution)/shard_map/ppermute | solution.py:367
  23.5 0.3 copy.15
  24.0 2.2 %shard_map.66.refs_0_ = bf16[1,8,128]{2,1,0:T(8,128)(2,1)S(1)} custom-call(bf16[8,1152]{1,0:T(8,128)(2,1)S(1)} %shard_map.65.own_ref, bf16[8,1152]{1,0:T(8,128)(2,1)S(1)} %collective-permute-done.4.up_ref, bf16[8,1152]{1,0:T(8,128)(2,1)S(1)} %collective-permute-done.5.down_ref, bf16[2,64,72]{2,1,0:T(8,128)(2,1)S(1)} %pad_maximum_fusion.w1_ref, ...), custom_call_target="tpu_custom_call" | custom-call | tf_op jit(solution)/shard_map/pallas_call | solution.py:371
  26.2 0.4 collective-permute-done.7.up_ref
  26.6 2.2 %shard_map.68.refs_1_ = bf16[1,8,128]{2,1,0:T(8,128)(2,1)S(1)} custom-call(bf16[8,1152]{1,0:T(8,128)(2,1)S(1)} %shard_map.67.own_ref, bf16[8,1152]{1,0:T(8,128)(2,1)S(1)} %collective-permute-done.7.up_ref, bf16[8,1152]{1,0:T(8,128)(2,1)S(1)} %collective-permute-done.8.down_ref, bf16[2,64,72]{2,1,0:T(8,128)(2,1)S(1)} %pad_maximum_fusion.w1_ref, ...), custom_call_target="tpu_custom_call" | custom-call | tf_op jit(solution)/shard_map/pallas_call | solution.py:371
  28.9 3.0 %shard_map.69 = bf16[64,3,8,128]{3,2,1,0:T(8,128)(2,1)} custom-call(bf16[8,1152]{1,0:T(8,128)(2,1)S(1)} %shard_map.64.own_ref, bf16[8,1152]{1,0:T(8,128)(2,1)S(1)} %collective-permute-done.1.up_ref, bf16[8,1152]{1,0:T(8,128)(2,1)S(1)} %collective-permute-done.2.down_ref, bf16[2,64,72]{2,1,0:T(8,128)(2,1)S(1)} %pad_maximum_fusion.w1_ref, ...), custom_call_target="tpu_custom_call" | custom-call | tf_op jit(solution)/shard_map/pallas_call | solution.py:371
  31.9 12.9 %all-to-all-start = ((bf16[64,3,8,128]{3,2,1,0:T(8,128)(2,1)}), bf16[64,3,8,128]{3,2,1,0:T(8,128)(2,1)S(1)}, u32[]{:S(2)}, u32[]{:S(2)}) async-start(bf16[64,3,8,128]{3,2,1,0:T(8,128)(2,1)} %shard_map.69), calls=%async_computation | async-start | bytes 786432 | tf_op jit(solution)/shard_map/all_to_all | solution.py:401
  44.9 0.6 copy.17.rows_ref
  45.5 1.9 %coef.1.coef_ref = f32[384]{0:T(512)} custom-call(s32[2,96]{1,0:T(2,128)} %bitcast.18, f32[2,96]{1,0:T(2,128)} %copy.17.rows_ref), custom_call_target="tpu_custom_call" | custom-call | flops 2000000 | bytes 4000000 | tf_op jit(solution)/shard_map/coef/pallas_call | solution.py:336
  47.4 15.6 %all-to-all-done.gathered_ref = bf16[64,3,8,128]{3,2,1,0:T(8,128)(2,1)S(1)} async-done(((bf16[64,3,8,128]{3,2,1,0:T(8,128)(2,1)}), bf16[64,3,8,128]{3,2,1,0:T(8,128)(2,1)S(1)}, u32[]{:S(2)}, u32[]{:S(2)}) %all-to-all-start) | async-done | bytes 393248 | tf_op jit(solution)/shard_map/all_to_all | solution.py:401
  63.0 1.5 %sums.1 = f32[2,8,256]{2,1,0:T(8,128)} custom-call(f32[384]{0:T(512)} %coef.1.coef_ref, bf16[64,3,8,128]{3,2,1,0:T(8,128)(2,1)S(1)} %all-to-all-done.gathered_ref), custom_call_target="tpu_custom_call" | custom-call | tf_op jit(solution)/shard_map/sums/pallas_call | solution.py:403
  (24 shorter events, 0.7 us)
Async XLA Ops:
  0.0 44.8 %copy-start = (f32[128,96]{0,1:T(8,128)S(1)}, f32[128,96]{0,1:T(8,128)}, u32[]{:S(2)}) copy-start(f32[128,96]{0,1:T(8,128)} %param.11) | copy-start | bytes 147460
  2.5 7.4 %copy-start.2 = (bf16[3,3,64,2]{2,3,1,0:T(2,128)(2,1)S(1)}, bf16[3,3,64,2]{2,3,1,0:T(2,128)(2,1)}, u32[]{:S(2)}) copy-start(bf16[3,3,64,2]{2,3,1,0:T(2,128)(2,1)} %param.8) | copy-start | bytes 6916
  2.6 14.3 %collective-permute-start.3 = (bf16[2,32,2176]{2,1,0:T(8,128)(2,1)S(1)}, bf16[2,32,2176]{2,1,0:T(8,128)(2,1)S(1)}, u32[]{:S(2)}, u32[]{:S(2)}) collective-permute-start(bf16[2,32,2176]{2,1,0:T(8,128)(2,1)S(1)} %get-tuple-element.17), channel_id=1, source_target_pairs={{0,4},{4,0},{8,12},{12,8},{16,20},{20,16},{24,28},{28,24},{32,36},... | collective-permute-start | bytes 835592 | tf_op jit(solution)/shard_map/ppermute | solution.py:333
  4.5 15.7 %collective-permute-start = (bf16[2,32,2176]{2,1,0:T(8,128)(2,1)S(1)}, bf16[2,32,2176]{2,1,0:T(8,128)(2,1)S(1)}, u32[]{:S(2)}, u32[]{:S(2)}) collective-permute-start(bf16[2,32,2176]{2,1,0:T(8,128)(2,1)S(1)} %get-tuple-element.15), channel_id=1, source_target_pairs={{0,8},{4,12},{8,0},{12,4},{16,24},{20,28},{24,16},{28,20},{32,40},... | collective-permute-start | bytes 835592 | tf_op jit(solution)/shard_map/ppermute | solution.py:333
  7.8 13.6 %collective-permute-start.6 = (bf16[2,32,2176]{2,1,0:T(8,128)(2,1)S(1)}, bf16[2,32,2176]{2,1,0:T(8,128)(2,1)S(1)}, u32[]{:S(2)}, u32[]{:S(2)}) collective-permute-start(bf16[2,32,2176]{2,1,0:T(8,128)(2,1)S(1)} %get-tuple-element.19), channel_id=1, source_target_pairs={{0,128},{4,132},{8,136},{12,140},{16,144},{20,148},{24,152},{28,15... | collective-permute-start | bytes 835592 | tf_op jit(solution)/shard_map/ppermute | solution.py:333
  17.5 5.9 %collective-permute-start.5 = (bf16[8,1152]{1,0:T(8,128)(2,1)S(1)}, bf16[8,1152]{1,0:T(8,128)(2,1)S(1)}, u32[]{:S(2)}, u32[]{:S(2)}) collective-permute-start(bf16[8,1152]{1,0:T(8,128)(2,1)S(1)} %shard_map.65.own_ref), channel_id=1, source_target_pairs={{1,0},{2,1},{3,2},{0,3},{5,4},{6,5},{7,6},{4,7},{9,8},{10,9},{11,1... | collective-permute-start | bytes 55304 | tf_op jit(solution)/shard_map/ppermute | solution.py:367
  17.6 0.7 %copy-start.3 = (bf16[3,3,1,64]{3,1,2,0:T(4,128)(2,1)S(1)}, bf16[3,3,1,64]{3,1,2,0:T(4,128)(2,1)}, u32[]{:S(2)}) copy-start(bf16[3,3,1,64]{3,1,2,0:T(4,128)(2,1)} %param.10) | copy-start | bytes 3460
  18.3 5.7 %collective-permute-start.4 = (bf16[8,1152]{1,0:T(8,128)(2,1)S(1)}, bf16[8,1152]{1,0:T(8,128)(2,1)S(1)}, u32[]{:S(2)}, u32[]{:S(2)}) collective-permute-start(bf16[8,1152]{1,0:T(8,128)(2,1)S(1)} %shard_map.65.own_ref), channel_id=1, source_target_pairs={{0,1},{1,2},{2,3},{3,0},{4,5},{5,6},{6,7},{7,4},{8,9},{9,10},{10,1... | collective-permute-start | bytes 55304 | tf_op jit(solution)/shard_map/ppermute | solution.py:366
  20.8 8.0 %collective-permute-start.2 = (bf16[8,1152]{1,0:T(8,128)(2,1)S(1)}, bf16[8,1152]{1,0:T(8,128)(2,1)S(1)}, u32[]{:S(2)}, u32[]{:S(2)}) collective-permute-start(bf16[8,1152]{1,0:T(8,128)(2,1)S(1)} %shard_map.64.own_ref), channel_id=1, source_target_pairs={{1,0},{2,1},{3,2},{0,3},{5,4},{6,5},{7,6},{4,7},{9,8},{10,9},{11,1... | collective-permute-start | bytes 55304 | tf_op jit(solution)/shard_map/ppermute | solution.py:367
  20.9 8.0 %collective-permute-start.1 = (bf16[8,1152]{1,0:T(8,128)(2,1)S(1)}, bf16[8,1152]{1,0:T(8,128)(2,1)S(1)}, u32[]{:S(2)}, u32[]{:S(2)}) collective-permute-start(bf16[8,1152]{1,0:T(8,128)(2,1)S(1)} %shard_map.64.own_ref), channel_id=1, source_target_pairs={{0,1},{1,2},{2,3},{3,0},{4,5},{5,6},{6,7},{7,4},{8,9},{9,10},{10,1... | collective-permute-start | bytes 55304 | tf_op jit(solution)/shard_map/ppermute | solution.py:366
  21.4 2.1 %copy-start.1 = (bf16[2,3,3,64,64]{4,3,2,1,0:T(8,128)(2,1)S(1)}, bf16[2,3,3,64,64]{4,3,2,1,0:T(8,128)(2,1)}, u32[]{:S(2)}) copy-start(bf16[2,3,3,64,64]{4,3,2,1,0:T(8,128)(2,1)} %param.9) | copy-start | bytes 442372
  22.0 4.2 %collective-permute-start.8 = (bf16[8,1152]{1,0:T(8,128)(2,1)S(1)}, bf16[8,1152]{1,0:T(8,128)(2,1)S(1)}, u32[]{:S(2)}, u32[]{:S(2)}) collective-permute-start(bf16[8,1152]{1,0:T(8,128)(2,1)S(1)} %shard_map.67.own_ref), channel_id=1, source_target_pairs={{1,0},{2,1},{3,2},{0,3},{5,4},{6,5},{7,6},{4,7},{9,8},{10,9},{11,1... | collective-permute-start | bytes 55304 | tf_op jit(solution)/shard_map/ppermute | solution.py:367
  23.5 3.2 %collective-permute-start.7 = (bf16[8,1152]{1,0:T(8,128)(2,1)S(1)}, bf16[8,1152]{1,0:T(8,128)(2,1)S(1)}, u32[]{:S(2)}, u32[]{:S(2)}) collective-permute-start(bf16[8,1152]{1,0:T(8,128)(2,1)S(1)} %shard_map.67.own_ref), channel_id=1, source_target_pairs={{0,1},{1,2},{2,3},{3,0},{4,5},{5,6},{6,7},{7,4},{8,9},{9,10},{10,1... | collective-permute-start | bytes 55304 | tf_op jit(solution)/shard_map/ppermute | solution.py:366
  31.9 31.1 %all-to-all-start = ((bf16[64,3,8,128]{3,2,1,0:T(8,128)(2,1)}), bf16[64,3,8,128]{3,2,1,0:T(8,128)(2,1)S(1)}, u32[]{:S(2)}, u32[]{:S(2)}) async-start(bf16[64,3,8,128]{3,2,1,0:T(8,128)(2,1)} %shard_map.69), calls=%async_computation | async-start | bytes 786432 | tf_op jit(solution)/shard_map/all_to_all | solution.py:401

commit v3 on v2

--- a/solution.py
+++ b/solution.py
@@ -19,7 +19,7 @@
 EXT = (STRIP_ROWS + 2 * HALO) * PITCH
 BITS = (0, 1, 5)
 SWAPS = (2, 1, 0)
-GROUPS = ((2,), (0,), (1,))
+GROUPS = ((2,), (0, 1))
 PART = 8 * PITCH
 SMEM = pltpu.SMEM
 VMEM = pltpu.VMEM
@@ -31,6 +31,13 @@
 
 def spec(space):
     return pl.BlockSpec(memory_space=space)
+
+
+def pieces(scenes_ref, date, start, target, sem):
+    width = target.shape[2]
+    copy = pltpu.make_async_copy(scenes_ref.at[:, date, :, pl.ds(start, width)], target, sem)
+    copy.start()
+    return [copy]
 
 
 def prep_kernel(pairs_ref, scenes_ref, *refs):
@@ -51,11 +58,7 @@
         local = (packed >> (2 * which)) & 1
         is_upper = (me >> BITS[which]) & 1
         start = pl.multiple_of((1 - is_upper) * (total - width), 128)
-        copy = pltpu.make_async_copy(
-            scenes_ref.at[:, local, :, pl.ds(start, width)], sends[slot], sems.at[slot]
-        )
-        copy.start()
-        copies.append(copy)
+        copies += pieces(scenes_ref, local, start, sends[slot], sems.at[slot])
         info_ref[2 * which] = local
         info_ref[2 * which + 1] = (packed >> (2 * which + 1)) & 1
     for copy in copies:
@@ -71,29 +74,27 @@
     for which, own in enumerate(owns):
         is_upper = (me >> BITS[which]) & 1
         start = pl.multiple_of(is_upper * (total - width), 128)
-        copy = pltpu.make_async_copy(
-            scenes_ref.at[:, info_ref[2 * which], :, pl.ds(start, width)], own, sems.at[which]
-        )
-        copy.start()
-        copies.append(copy)
+        copies += pieces(scenes_ref, info_ref[2 * which], start, own, sems.at[which])
         sign = jnp.where(info_ref[2 * which + 1] == 1, 1.0, -1.0).astype(F32)
         sign_ref[which] = jnp.full(sign_ref.shape[1:], sign, F32)
     for copy in copies:
         copy.wait()
 
 
-def coef_kernel(pairs_ref, rows_ref, coef_ref):
+def coef_kernel(pairs_ref, inversion_ref, coef_ref):
+    me = lax.axis_index("date")
     block = pairs_ref.shape[1] // 3
     groups = 2 * block
+    dates = (2 * me, 2 * me + 1, 2 * (me ^ block), 2 * (me ^ block) + 1)
     for which in range(3):
 
         def step(slot, carry):
             pair = which * block + slot
             first = pairs_ref[0, pair] >> 1
             second = pairs_ref[1, pair] >> 1
-            for date in range(2):
-                value = rows_ref[date, pair]
-                base = (which * 2 + date) * groups
+            for place, date in enumerate(dates):
+                value = inversion_ref[pair, date]
+                base = (which * 4 + place) * groups
                 coef_ref[base + first] = value
                 coef_ref[base + second] = value
             return carry
@@ -236,19 +237,22 @@
         )
         return to_even, to_odd
 
-    for slot, which in enumerate(matchings):
+    slots = range(len(matchings))
+    for slot in slots:
         for part, (lo, hi) in enumerate(((128, 1152), (0, 1024))):
             base = part * PART
             value = jnp.dot(
                 w1_ref[slot], taps[:, base + lo : base + hi], preferred_element_type=F32
             )
-            hidden_a[part, :, guard + lo : guard + hi] = masked(value, part, lo, hi)
-        outs = ((128, 1024), (128, 1024))
-        both = joined(hidden_a, w2_ref[0], ((128, 1152), (0, 1024)), outs)
+            hidden_a[slot, part, :, guard + lo : guard + hi] = masked(value, part, lo, hi)
+    outs = ((128, 1024), (128, 1024))
+    for slot in slots:
+        both = joined(hidden_a.at[slot], w2_ref[0], ((128, 1152), (0, 1024)), outs)
         for part, (lo, hi) in enumerate(outs):
-            hidden_b[part, :, guard + lo : guard + hi] = masked(both[part], part, lo, hi)
-        outs = ((256, 1024), (128, 896))
-        both = joined(hidden_b, w2_ref[1], ((128, 1024), (128, 1024)), outs)
+            hidden_b[slot, part, :, guard + lo : guard + hi] = masked(both[part], part, lo, hi)
+    outs = ((256, 1024), (128, 896))
+    for slot, which in enumerate(matchings):
+        both = joined(hidden_b.at[slot], w2_ref[1], ((128, 1024), (128, 1024)), outs)
         is_upper = (me >> BITS[which]) & 1
         for part, (lo, hi) in enumerate(outs):
             value = masked(both[part], part, lo, hi)
@@ -258,7 +262,8 @@
                 + value[8:16]
                 + pltpu.roll(value[16:24], hi - lo - 1, 1)
             )
-            zs[part] = jnp.where(is_upper == 1, pltpu.roll(value, hi - lo - 8, 1), value)
+            zs[slot, part] = jnp.where(is_upper == 1, pltpu.roll(value, hi - lo - 8, 1), value)
+    for slot, which in enumerate(matchings):
         for r in range(STRIP_ROWS):
             at = (r // 2 + HALO // 2) * PITCH
             if r % 2 == 0:
@@ -268,10 +273,10 @@
             total = None
             for part, p, move in picks:
                 start = at + move - outs[part][0]
-                value = zs[part, p : p + 1, start : start + 128]
+                value = zs[slot, part, p : p + 1, start : start + 128]
                 total = value if total is None else total + value
-            phases[r : r + 1, :] = total
-        phase = phases[...].astype(BF)
+            phases[slot, r : r + 1, :] = total
+        phase = phases[slot].astype(BF)
         if len(out_ref.shape) == 3:
             out_ref[slot] = phase
         else:
@@ -285,25 +290,34 @@
                 out_ref[target, which] = phase
 
 
-def sum_kernel(coef_ref, gathered_ref, out_ref):
-    groups = gathered_ref.shape[0]
-    acc = [[jnp.zeros((8, 128), F32) for _ in range(2)] for _ in range(2)]
-    for group in range(groups):
+def sum_kernel(coef_ref, gathered_ref, mine_ref, other_ref):
+    me = lax.axis_index("date")
+    half = gathered_ref.shape[0]
+    groups = 2 * half
+    is_upper = me // half
+    zero = jnp.zeros((8, 128), F32)
+    sides = [[zero, zero] for _ in range(4)]
+    own_side = [zero] * 4
+    for source in range(half):
         for which in range(3):
-            side = group >> BITS[which] & 1
-            phase = gathered_ref[group, which].astype(F32)
-            for date in range(2):
-                coef = coef_ref[(which * 2 + date) * groups + group]
-                acc[date][side] = acc[date][side] + coef * phase
-    for date in range(2):
+            phase = gathered_ref[source, which].astype(F32)
+            for place in range(4):
+                coef = coef_ref[(which * 4 + place) * groups + is_upper * half + source]
+                if which == 2:
+                    own_side[place] = own_side[place] + coef * phase
+                else:
+                    side = source >> BITS[which] & 1
+                    sides[place][side] = sides[place][side] + coef * phase
+    for place in range(4):
+        out = mine_ref if place < 2 else other_ref
         for side in range(2):
-            out_ref[date, :, side * 128 : side * 128 + 128] = acc[date][side]
+            value = sides[place][side] + jnp.where(is_upper == side, own_side[place], zero)
+            out[place % 2, :, side * 128 : side * 128 + 128] = value
 
 
 def per_device(scenes, date_pairs, first_weight, mid_weight, last_weight, inversion):
     groups = lax.axis_size("date")
     strips = lax.axis_size("strip")
-    me = lax.axis_index("date").astype(jnp.int32)
     width = PIECE_COLS * LOOK_C
     rows = scenes.shape[2]
     ch = first_weight.shape[2]
@@ -332,15 +346,14 @@
         route = [(low, low ^ 1 << BITS[which]) for low in range(groups)]
         recvs[which] = lax.ppermute(sends[slot], "date", route)
 
-    own_rows = lax.dynamic_slice_in_dim(inversion, 2 * me, 2, axis=0)
     coef = pl.pallas_call(
         coef_kernel,
         name="coef",
-        out_shape=jax.ShapeDtypeStruct((6 * groups,), F32),
+        out_shape=jax.ShapeDtypeStruct((12 * groups,), F32),
         in_specs=[spec(SMEM), spec(SMEM)],
         out_specs=spec(SMEM),
         cost_estimate=pl.CostEstimate(flops=2000000, bytes_accessed=4000000, transcendentals=0),
-    )(pairs, own_rows)
+    )(pairs, inversion.T)
 
     w1 = jnp.transpose(first_weight, (2, 0, 1, 3)).reshape(ch, 9, 2)
     w1 = jnp.stack(
@@ -376,11 +389,11 @@
             scratch_shapes=[
                 pltpu.VMEM((8, EXT), F32),
                 pltpu.VMEM((72, EXT), BF),
-                pltpu.VMEM((2, ch, PART + 256), BF),
-                pltpu.VMEM((2, ch, PART + 256), BF),
-                pltpu.VMEM((2, 8, 768), F32),
+                pltpu.VMEM((len(matchings), 2, ch, PART + 256), BF),
+                pltpu.VMEM((len(matchings), 2, ch, PART + 256), BF),
+                pltpu.VMEM((len(matchings), 2, 8, 768), F32),
                 pltpu.VMEM((8, EXT), F32),
-                pltpu.VMEM((8, 128), F32),
+                pltpu.VMEM((len(matchings), 8, 128), F32),
             ],
         )(
             *[in_vmem(v) for v in looked], *[in_vmem(v) for v in (w1, w2, w4)],
@@ -395,18 +408,22 @@
             done.append(phases_of(group, value, shape))
     by_matching = {group[0]: value for group, value in zip(GROUPS, done)}
     rest = [by_matching[which] for which in sorted(by_matching)]
-    shape = (groups, 3, STRIP_ROWS, 128)
+    half = groups // 2
+    shape = (half, 3, STRIP_ROWS, 128)
     phases = phases_of(GROUPS[-1], looked[-1], shape, *rest)
 
-    gathered = lax.all_to_all(phases, "date", 0, 0, tiled=True)
-
-    return pl.pallas_call(
+    halves = [list(range(half)), list(range(half, groups))]
+    gathered = lax.all_to_all(phases, "date", 0, 0, tiled=True, axis_index_groups=halves)
+
+    mine, other = pl.pallas_call(
         sum_kernel,
         name="sums",
-        out_shape=jax.ShapeDtypeStruct((2, STRIP_ROWS, 256), F32),
+        out_shape=[pltpu.VMEM((2, STRIP_ROWS, 256), F32)] * 2,
         in_specs=[spec(SMEM), spec(VMEM)],
-        out_specs=spec(VMEM),
+        out_specs=[spec(VMEM)] * 2,
     )(coef, in_vmem(gathered))
+    route = [(low, low ^ half) for low in range(groups)]
+    return mine + lax.ppermute(other, "date", route)
 
 
 def solution(mesh):

time: 65.7 us -> 62.2 us (0.947)
  starting transfers between devices: 22.9 us -> 21.5 us
  local copies, waits for them, and re-layouts: 2.11 us -> 0.73 us
  waiting for transfers between devices: 21.9 us -> 21.2 us
    all_to_all x1, waiting for transfers between devices: 15.6 us -> 7.46 us  [per_device(): lax.all_to_all(phases, 'date', 0, 0, tiled=True, axis_index_groups=halves)]
    ppermute x0 -> x1, waiting for transfers between devices: none -> 3.05 us  [per_device(): return mine + lax.ppermute(other, 'date', route)]
    all_to_all x1, starting transfers between devices: 12.9 us -> 9.97 us  [per_device(): lax.all_to_all(phases, 'date', 0, 0, tiled=True, axis_index_groups=halves)]
    ppermute x0 -> x1, starting transfers between devices: none -> 2.28 us  [per_device(): return mine + lax.ppermute(other, 'date', route)]
    ppermute x3, waiting for transfers between devices: 5.89 us -> 8.04 us  [per_device(): recvs[which] = lax.ppermute(sends[slot], 'date', route)]
    pallas_call x1, Pallas kernels: 1.87 us -> 3.27 us  [per_device(): pl.pallas_call(coef_kernel, name='coef', out_shape=jax.ShapeDtypeStruct((...]
    ppermute x3 -> x2, waiting for transfers between devices: 0.41 us -> 1.73 us  [looked_of(): lax.ppermute(looked, 'strip', [(i, (i + 1) % strips) for i in range(strip...]
    unnamed x10 -> x7, local copies, waits for them, and re-layouts: 1.32 us -> 0.02 us
  transfers between devices with their start and end apart: 10 -> 9, of which waited for: 4 -> 6; matrix products, arithmetic and copies ran while one was open for 2% -> 1% of each run, Pallas kernels for 16% -> 15%
where the time goes in v3:
time: 62.2 us; the launch traced here: 61.3 us
  starting transfers between devices  21.5 us (35%)
  waiting for transfers between devices  21.2 us (34%)
  Pallas kernels  17.1 us (27%)
  local copies, waits for them, and re-layouts  0.73 us (1%)
    all_to_all x1, starting transfers between devices, per_device(): lax.all_to_all(phases, 'date', 0, 0, tiled=True, axis_index_groups=halves)  9.97 us
    ppermute x3, waiting for transfers between devices, per_device(): recvs[which] = lax.ppermute(sends[slot], 'date', route)  8.04 us
    all_to_all x1, waiting for transfers between devices, per_device(): lax.all_to_all(phases, 'date', 0, 0, tiled=True, axis_index_groups=halves)  7.46 us
    ppermute x3, starting transfers between devices, per_device(): recvs[which] = lax.ppermute(sends[slot], 'date', route)  7.27 us
    pallas_call x2, Pallas kernels, phases_of(): pl.pallas_call(functools.partial(conv_kernel, matchings), out_shape=pltpu...  6.69 us
    pallas_call x1, Pallas kernels, per_device(): pl.pallas_call(coef_kernel, name='coef', out_shape=jax.ShapeDtypeStruct((...  3.27 us
    ppermute x1, waiting for transfers between devices, per_device(): return mine + lax.ppermute(other, 'date', route)  3.05 us
    pallas_call x1, Pallas kernels, per_device(): pl.pallas_call(prep_kernel, name='prep', out_shape=[pltpu.VMEM(piece, BF)...  2.6 us
  transfers between devices with their start and end apart: 9, of which 6 were waited for; matrix products, arithmetic and copies ran while one was open for 1% of the time, Pallas kernels for 15%

profile of v3, /device:TPU:2, one launch (start us, length us, event | category | flops | bytes accessed | tf_op | source)
XLA Modules:
  0.0 61.3 jit_solution(17134716366853091010)
XLA Ops:
  0.0 2.6 %prep.1 = (bf16[2,32,2176]{2,1,0:T(8,128)(2,1)S(1)}, bf16[2,32,2176]{2,1,0:T(8,128)(2,1)S(1)}, bf16[2,32,2176]{2,1,0:T(8,128)(2,1)S(1)}, s32[8]{0:T(128)}) custom-call(s32[2,96]{1,0:T(2,128)} %bitcast.18, bf16[2,2,32,4096]{3,2,1,0:T(8,128)(2,1)} %scenes_ref.3), custom_call_target="tpu_custom_call" | custom-call | tf_op jit(solution)/shard_map/prep/pallas_call | solution.py:327
  2.6 1.9 %collective-permute-start = (bf16[2,32,2176]{2,1,0:T(8,128)(2,1)S(1)}, bf16[2,32,2176]{2,1,0:T(8,128)(2,1)S(1)}, u32[]{:S(2)}, u32[]{:S(2)}) collective-permute-start(bf16[2,32,2176]{2,1,0:T(8,128)(2,1)S(1)} %get-tuple-element.17), channel_id=1, source_target_pairs={{0,4},{4,0},{8,12},{12,8},{16,20},{20,16},{24,28},{28,24},{32,36},... | collective-permute-start | bytes 835592 | tf_op jit(solution)/shard_map/ppermute | solution.py:347
  4.5 3.3 %collective-permute-start.1 = (bf16[2,32,2176]{2,1,0:T(8,128)(2,1)S(1)}, bf16[2,32,2176]{2,1,0:T(8,128)(2,1)S(1)}, u32[]{:S(2)}, u32[]{:S(2)}) collective-permute-start(bf16[2,32,2176]{2,1,0:T(8,128)(2,1)S(1)} %get-tuple-element.18), channel_id=1, source_target_pairs={{0,8},{4,12},{8,0},{12,4},{16,24},{20,28},{24,16},{28,20},{32,40},... | collective-permute-start | bytes 835592 | tf_op jit(solution)/shard_map/ppermute | solution.py:347
  7.8 2.1 %collective-permute-start.4 = (bf16[2,32,2176]{2,1,0:T(8,128)(2,1)S(1)}, bf16[2,32,2176]{2,1,0:T(8,128)(2,1)S(1)}, u32[]{:S(2)}, u32[]{:S(2)}) collective-permute-start(bf16[2,32,2176]{2,1,0:T(8,128)(2,1)S(1)} %get-tuple-element.21), channel_id=1, source_target_pairs={{0,128},{4,132},{8,136},{12,140},{16,144},{20,148},{24,152},{28,15... | collective-permute-start | bytes 835592 | tf_op jit(solution)/shard_map/ppermute | solution.py:347
  10.1 2.0 %own.1 = (bf16[2,32,2176]{2,1,0:T(8,128)(2,1)S(1)}, bf16[2,32,2176]{2,1,0:T(8,128)(2,1)S(1)}, bf16[2,32,2176]{2,1,0:T(8,128)(2,1)S(1)}, f32[3,8,128]{2,1,0:T(8,128)S(1)}) custom-call(s32[8]{0:T(128)} %get-tuple-element.15.info_ref, bf16[2,2,32,4096]{3,2,1,0:T(8,128)(2,1)} %scenes_ref.3), custom_call_target="tpu_custom_call" | custom-call | tf_op jit(solution)/shard_map/own/pallas_call | solution.py:335
  12.1 4.8 %collective-permute-done.refs_0_ = bf16[2,32,2176]{2,1,0:T(8,128)(2,1)S(1)} collective-permute-done((bf16[2,32,2176]{2,1,0:T(8,128)(2,1)S(1)}, bf16[2,32,2176]{2,1,0:T(8,128)(2,1)S(1)}, u32[]{:S(2)}, u32[]{:S(2)}) %collective-permute-start) | collective-permute-done | bytes 278560 | tf_op jit(solution)/shard_map/ppermute | solution.py:347
  16.9 3.3 %collective-permute-done.1.refs_1_ = bf16[2,32,2176]{2,1,0:T(8,128)(2,1)S(1)} collective-permute-done((bf16[2,32,2176]{2,1,0:T(8,128)(2,1)S(1)}, bf16[2,32,2176]{2,1,0:T(8,128)(2,1)S(1)}, u32[]{:S(2)}, u32[]{:S(2)}) %collective-permute-start.1) | collective-permute-done | bytes 278560 | tf_op jit(solution)/shard_map/ppermute | solution.py:347
  20.2 1.0 %shard_map.64.own_ref = bf16[8,1152]{1,0:T(8,128)(2,1)S(1)} custom-call(f32[3,8,128]{2,1,0:T(8,128)S(1)} %get-tuple-element.16.sign_ref, bf16[2,32,2176]{2,1,0:T(8,128)(2,1)S(1)} %collective-permute-done.refs_0_, bf16[2,32,2176]{2,1,0:T(8,128)(2,1)S(1)} %collective-permute-done.1.refs_1_, bf16[2,32,2176]{2,1,0:T(8,128)(2,1)S(1)} %get-tuple-element.19.refs_2_, ...), custom_call_target="tpu_custom_call" | custom-call | tf_op jit(solution)/shard_map/pallas_call | solution.py:368
  21.2 0.5 collective-permute-start.2
  21.8 0.6 %shard_map.65.own_ref = bf16[8,1152]{1,0:T(8,128)(2,1)S(1)} custom-call(f32[3,8,128]{2,1,0:T(8,128)S(1)} %get-tuple-element.16.sign_ref, bf16[2,32,2176]{2,1,0:T(8,128)(2,1)S(1)} %collective-permute-done.4.refs_0_, bf16[2,32,2176]{2,1,0:T(8,128)(2,1)S(1)} %get-tuple-element.22.refs_1_), custom_call_target="tpu_custom_call" | custom-call | tf_op jit(solution)/shard_map/pallas_call | solution.py:368
  22.4 1.4 %collective-permute-start.6 = (bf16[8,1152]{1,0:T(8,128)(2,1)S(1)}, bf16[8,1152]{1,0:T(8,128)(2,1)S(1)}, u32[]{:S(2)}, u32[]{:S(2)}) collective-permute-start(bf16[8,1152]{1,0:T(8,128)(2,1)S(1)} %shard_map.65.own_ref), channel_id=1, source_target_pairs={{1,0},{2,1},{3,2},{0,3},{5,4},{6,5},{7,6},{4,7},{9,8},{10,9},{11,1... | collective-permute-start | bytes 55304 | tf_op jit(solution)/shard_map/ppermute | solution.py:380
  23.8 0.3 copy.13
  24.1 0.2 reshape.10.w2_ref
  24.3 0.9 %collective-permute-done.6.down_ref = bf16[8,1152]{1,0:T(8,128)(2,1)S(1)} collective-permute-done((bf16[8,1152]{1,0:T(8,128)(2,1)S(1)}, bf16[8,1152]{1,0:T(8,128)(2,1)S(1)}, u32[]{:S(2)}, u32[]{:S(2)}) %collective-permute-start.6) | collective-permute-done | bytes 18464 | tf_op jit(solution)/shard_map/ppermute | solution.py:380
  25.3 1.7 %collective-permute-done.5.up_ref = bf16[8,1152]{1,0:T(8,128)(2,1)S(1)} collective-permute-done((bf16[8,1152]{1,0:T(8,128)(2,1)S(1)}, bf16[8,1152]{1,0:T(8,128)(2,1)S(1)}, u32[]{:S(2)}, u32[]{:S(2)}) %collective-permute-start.5) | collective-permute-done | bytes 18464 | tf_op jit(solution)/shard_map/ppermute | solution.py:379
  27.0 2.2 %shard_map.66.refs_0_ = bf16[1,8,128]{2,1,0:T(8,128)(2,1)S(1)} custom-call(bf16[8,1152]{1,0:T(8,128)(2,1)S(1)} %shard_map.65.own_ref, bf16[8,1152]{1,0:T(8,128)(2,1)S(1)} %collective-permute-done.5.up_ref, bf16[8,1152]{1,0:T(8,128)(2,1)S(1)} %collective-permute-done.6.down_ref, bf16[2,64,72]{2,1,0:T(8,128)(2,1)S(1)} %pad_maximum_fusion.w1_ref, ...), custom_call_target="tpu_custom_call" | custom-call | tf_op jit(solution)/shard_map/pallas_call | solution.py:384
  29.2 4.5 %shard_map.67 = bf16[32,3,8,128]{3,2,1,0:T(8,128)(2,1)} custom-call(bf16[8,1152]{1,0:T(8,128)(2,1)S(1)} %shard_map.64.own_ref, bf16[8,1152]{1,0:T(8,128)(2,1)S(1)} %collective-permute-done.2.up_ref, bf16[8,1152]{1,0:T(8,128)(2,1)S(1)} %collective-permute-done.3.down_ref, bf16[2,64,72]{2,1,0:T(8,128)(2,1)S(1)} %pad_maximum_fusion.w1_ref, ...), custom_call_target="tpu_custom_call" | custom-call | tf_op jit(solution)/shard_map/pallas_call | solution.py:384
  33.7 10.0 %all-to-all-start = ((bf16[32,3,8,128]{3,2,1,0:T(8,128)(2,1)}), bf16[32,3,8,128]{3,2,1,0:T(8,128)(2,1)S(1)}, u32[]{:S(2)}, u32[]{:S(2)}) async-start(bf16[32,3,8,128]{3,2,1,0:T(8,128)(2,1)} %shard_map.67), calls=%async_computation | async-start | bytes 393216 | tf_op jit(solution)/shard_map/all_to_all | solution.py:416
  43.7 3.3 %coef.1.coef_ref = f32[768]{0:T(1024)} custom-call(s32[2,96]{1,0:T(2,128)} %bitcast.19, f32[96,128]{1,0:T(8,128)} %bitcast.16), custom_call_target="tpu_custom_call" | custom-call | flops 2000000 | bytes 4000000 | tf_op jit(solution)/shard_map/coef/pallas_call | solution.py:349
  47.0 7.5 %all-to-all-done.gathered_ref = bf16[32,3,8,128]{3,2,1,0:T(8,128)(2,1)S(1)} async-done(((bf16[32,3,8,128]{3,2,1,0:T(8,128)(2,1)}), bf16[32,3,8,128]{3,2,1,0:T(8,128)(2,1)S(1)}, u32[]{:S(2)}, u32[]{:S(2)}) %all-to-all-start) | async-done | bytes 196640 | tf_op jit(solution)/shard_map/all_to_all | solution.py:416
  54.4 0.9 %sums.1 = (f32[2,8,256]{2,1,0:T(8,128)S(1)}, f32[2,8,256]{2,1,0:T(8,128)S(1)}) custom-call(f32[768]{0:T(1024)} %coef.1.coef_ref, bf16[32,3,8,128]{3,2,1,0:T(8,128)(2,1)S(1)} %all-to-all-done.gathered_ref), custom_call_target="tpu_custom_call" | custom-call | tf_op jit(solution)/shard_map/sums/pallas_call | solution.py:418
  55.4 2.3 %collective-permute-start.7 = (f32[2,8,256]{2,1,0:T(8,128)S(1)}, f32[2,8,256]{2,1,0:T(8,128)S(1)}, u32[]{:S(2)}, u32[]{:S(2)}) collective-permute-start(f32[2,8,256]{2,1,0:T(8,128)S(1)} %get-tuple-element.24), channel_id=1, source_target_pairs={{0,128},{4,132},{8,136},{12,140},{16,144},{20,148},{24,152},{28,15... | collective-permute-start | bytes 49160 | tf_op jit(solution)/shard_map/ppermute | solution.py:426
  57.6 3.0 %collective-permute-done.7 = f32[2,8,256]{2,1,0:T(8,128)S(1)} collective-permute-done((f32[2,8,256]{2,1,0:T(8,128)S(1)}, f32[2,8,256]{2,1,0:T(8,128)S(1)}, u32[]{:S(2)}, u32[]{:S(2)}) %collective-permute-start.7) | collective-permute-done | bytes 16416 | tf_op jit(solution)/shard_map/ppermute | solution.py:426
  60.7 0.6 add.9
  (17 shorter events, 0.3 us)
Async XLA Ops:
  2.6 7.3 %copy-start.2 = (bf16[3,3,1,64]{3,1,2,0:T(4,128)(2,1)S(1)}, bf16[3,3,1,64]{3,1,2,0:T(4,128)(2,1)}, u32[]{:S(2)}) copy-start(bf16[3,3,1,64]{3,1,2,0:T(4,128)(2,1)} %param.10) | copy-start | bytes 3460
  2.6 14.3 %collective-permute-start = (bf16[2,32,2176]{2,1,0:T(8,128)(2,1)S(1)}, bf16[2,32,2176]{2,1,0:T(8,128)(2,1)S(1)}, u32[]{:S(2)}, u32[]{:S(2)}) collective-permute-start(bf16[2,32,2176]{2,1,0:T(8,128)(2,1)S(1)} %get-tuple-element.17), channel_id=1, source_target_pairs={{0,4},{4,0},{8,12},{12,8},{16,20},{20,16},{24,28},{28,24},{32,36},... | collective-permute-start | bytes 835592 | tf_op jit(solution)/shard_map/ppermute | solution.py:347
  4.5 15.7 %collective-permute-start.1 = (bf16[2,32,2176]{2,1,0:T(8,128)(2,1)S(1)}, bf16[2,32,2176]{2,1,0:T(8,128)(2,1)S(1)}, u32[]{:S(2)}, u32[]{:S(2)}) collective-permute-start(bf16[2,32,2176]{2,1,0:T(8,128)(2,1)S(1)} %get-tuple-element.18), channel_id=1, source_target_pairs={{0,8},{4,12},{8,0},{12,4},{16,24},{20,28},{24,16},{28,20},{32,40},... | collective-permute-start | bytes 835592 | tf_op jit(solution)/shard_map/ppermute | solution.py:347
  7.8 2.1 %copy-start.1 = (bf16[3,3,64,2]{2,3,1,0:T(2,128)(2,1)S(1)}, bf16[3,3,64,2]{2,3,1,0:T(2,128)(2,1)}, u32[]{:S(2)}) copy-start(bf16[3,3,64,2]{2,3,1,0:T(2,128)(2,1)} %param.8) | copy-start | bytes 6916
  7.8 14.0 %collective-permute-start.4 = (bf16[2,32,2176]{2,1,0:T(8,128)(2,1)S(1)}, bf16[2,32,2176]{2,1,0:T(8,128)(2,1)S(1)}, u32[]{:S(2)}, u32[]{:S(2)}) collective-permute-start(bf16[2,32,2176]{2,1,0:T(8,128)(2,1)S(1)} %get-tuple-element.21), channel_id=1, source_target_pairs={{0,128},{4,132},{8,136},{12,140},{16,144},{20,148},{24,152},{28,15... | collective-permute-start | bytes 835592 | tf_op jit(solution)/shard_map/ppermute | solution.py:347
  21.2 8.0 %collective-permute-start.3 = (bf16[8,1152]{1,0:T(8,128)(2,1)S(1)}, bf16[8,1152]{1,0:T(8,128)(2,1)S(1)}, u32[]{:S(2)}, u32[]{:S(2)}) collective-permute-start(bf16[8,1152]{1,0:T(8,128)(2,1)S(1)} %shard_map.64.own_ref), channel_id=1, source_target_pairs={{1,0},{2,1},{3,2},{0,3},{5,4},{6,5},{7,6},{4,7},{9,8},{10,9},{11,1... | collective-permute-start | bytes 55304 | tf_op jit(solution)/shard_map/ppermute | solution.py:380
  21.2 8.0 %collective-permute-start.2 = (bf16[8,1152]{1,0:T(8,128)(2,1)S(1)}, bf16[8,1152]{1,0:T(8,128)(2,1)S(1)}, u32[]{:S(2)}, u32[]{:S(2)}) collective-permute-start(bf16[8,1152]{1,0:T(8,128)(2,1)S(1)} %shard_map.64.own_ref), channel_id=1, source_target_pairs={{0,1},{1,2},{2,3},{3,0},{4,5},{5,6},{6,7},{7,4},{8,9},{9,10},{10,1... | collective-permute-start | bytes 55304 | tf_op jit(solution)/shard_map/ppermute | solution.py:379
  21.7 2.1 %copy-start = (bf16[2,3,3,64,64]{4,3,2,1,0:T(8,128)(2,1)S(1)}, bf16[2,3,3,64,64]{4,3,2,1,0:T(8,128)(2,1)}, u32[]{:S(2)}) copy-start(bf16[2,3,3,64,64]{4,3,2,1,0:T(8,128)(2,1)} %param.9) | copy-start | bytes 442372
  22.4 2.9 %collective-permute-start.6 = (bf16[8,1152]{1,0:T(8,128)(2,1)S(1)}, bf16[8,1152]{1,0:T(8,128)(2,1)S(1)}, u32[]{:S(2)}, u32[]{:S(2)}) collective-permute-start(bf16[8,1152]{1,0:T(8,128)(2,1)S(1)} %shard_map.65.own_ref), channel_id=1, source_target_pairs={{1,0},{2,1},{3,2},{0,3},{5,4},{6,5},{7,6},{4,7},{9,8},{10,9},{11,1... | collective-permute-start | bytes 55304 | tf_op jit(solution)/shard_map/ppermute | solution.py:380
  23.8 3.2 %collective-permute-start.5 = (bf16[8,1152]{1,0:T(8,128)(2,1)S(1)}, bf16[8,1152]{1,0:T(8,128)(2,1)S(1)}, u32[]{:S(2)}, u32[]{:S(2)}) collective-permute-start(bf16[8,1152]{1,0:T(8,128)(2,1)S(1)} %shard_map.65.own_ref), channel_id=1, source_target_pairs={{0,1},{1,2},{2,3},{3,0},{4,5},{5,6},{6,7},{7,4},{8,9},{9,10},{10,1... | collective-permute-start | bytes 55304 | tf_op jit(solution)/shard_map/ppermute | solution.py:379
  33.7 20.7 %all-to-all-start = ((bf16[32,3,8,128]{3,2,1,0:T(8,128)(2,1)}), bf16[32,3,8,128]{3,2,1,0:T(8,128)(2,1)S(1)}, u32[]{:S(2)}, u32[]{:S(2)}) async-start(bf16[32,3,8,128]{3,2,1,0:T(8,128)(2,1)} %shard_map.67), calls=%async_computation | async-start | bytes 393216 | tf_op jit(solution)/shard_map/all_to_all | solution.py:416
  55.4 5.3 %collective-permute-start.7 = (f32[2,8,256]{2,1,0:T(8,128)S(1)}, f32[2,8,256]{2,1,0:T(8,128)S(1)}, u32[]{:S(2)}, u32[]{:S(2)}) collective-permute-start(f32[2,8,256]{2,1,0:T(8,128)S(1)} %get-tuple-element.24), channel_id=1, source_target_pairs={{0,128},{4,132},{8,136},{12,140},{16,144},{20,148},{24,152},{28,15... | collective-permute-start | bytes 49160 | tf_op jit(solution)/shard_map/ppermute | solution.py:426

commit v4 on v3

--- a/solution.py
+++ b/solution.py
@@ -40,9 +40,7 @@
     return [copy]
 
 
-def prep_kernel(pairs_ref, scenes_ref, *refs):
-    *sends, info_ref, sems = refs
-    me = lax.axis_index("date")
+def packed_dates(pairs_ref, me):
     both = pairs_ref[...]
     block = both.shape[1] // 3
     lane = lax.broadcasted_iota(jnp.int32, both.shape, 1)
@@ -50,7 +48,13 @@
     code = (both & 1) + jnp.where(side == 0, 2, 0)
     weight = jnp.where(lane < block, 1, jnp.where(lane < 2 * block, 4, 16))
     code = jnp.where((both >> 1) == me, code * weight, 0).astype(F32)
-    packed = jnp.sum(code).astype(jnp.int32)
+    return jnp.sum(code).astype(jnp.int32)
+
+
+def prep_kernel(pairs_ref, scenes_ref, *refs):
+    *sends, sems = refs
+    me = lax.axis_index("date")
+    packed = packed_dates(pairs_ref, me)
     width = sends[0].shape[2]
     total = scenes_ref.shape[3]
     copies = []
@@ -59,23 +63,24 @@
         is_upper = (me >> BITS[which]) & 1
         start = pl.multiple_of((1 - is_upper) * (total - width), 128)
         copies += pieces(scenes_ref, local, start, sends[slot], sems.at[slot])
-        info_ref[2 * which] = local
-        info_ref[2 * which + 1] = (packed >> (2 * which + 1)) & 1
     for copy in copies:
         copy.wait()
 
 
-def own_kernel(info_ref, scenes_ref, *refs):
+def own_kernel(pairs_ref, scenes_ref, *refs):
     *owns, sign_ref, sems = refs
     me = lax.axis_index("date")
+    packed = packed_dates(pairs_ref, me)
     width = owns[0].shape[2]
     total = scenes_ref.shape[3]
     copies = []
     for which, own in enumerate(owns):
         is_upper = (me >> BITS[which]) & 1
         start = pl.multiple_of(is_upper * (total - width), 128)
-        copies += pieces(scenes_ref, info_ref[2 * which], start, own, sems.at[which])
-        sign = jnp.where(info_ref[2 * which + 1] == 1, 1.0, -1.0).astype(F32)
+        local = (packed >> (2 * which)) & 1
+        copies += pieces(scenes_ref, local, start, own, sems.at[which])
+        is_ref = (packed >> (2 * which + 1)) & 1
+        sign = jnp.where(is_ref == 1, 1.0, -1.0).astype(F32)
         sign_ref[which] = jnp.full(sign_ref.shape[1:], sign, F32)
     for copy in copies:
         copy.wait()
@@ -324,22 +329,22 @@
     pairs = date_pairs.T
 
     piece = (2, rows, width)
-    *sends, info = pl.pallas_call(
+    sends = pl.pallas_call(
         prep_kernel,
         name="prep",
-        out_shape=[pltpu.VMEM(piece, BF)] * 3 + [jax.ShapeDtypeStruct((8,), jnp.int32)],
+        out_shape=[pltpu.VMEM(piece, BF)] * 3,
         in_specs=[spec(VMEM), spec(pl.ANY)],
-        out_specs=[spec(VMEM)] * 3 + [spec(SMEM)],
+        out_specs=[spec(VMEM)] * 3,
         scratch_shapes=[pltpu.SemaphoreType.DMA((3,))],
     )(pairs, scenes)
     *owns, signs = pl.pallas_call(
         own_kernel,
         name="own",
         out_shape=[pltpu.VMEM(piece, BF)] * 3 + [pltpu.VMEM((3, 8, 128), F32)],
-        in_specs=[spec(SMEM), spec(pl.ANY)],
+        in_specs=[spec(VMEM), spec(pl.ANY)],
         out_specs=[spec(VMEM)] * 4,
         scratch_shapes=[pltpu.SemaphoreType.DMA((3,))],
-    )(info, scenes)
+    )(pairs, scenes)
 
     recvs = {}
     for slot, which in enumerate(SWAPS):
@@ -349,7 +354,7 @@
     coef = pl.pallas_call(
         coef_kernel,
         name="coef",
-        out_shape=jax.ShapeDtypeStruct((12 * groups,), F32),
+        out_shape=pltpu.SMEM((12 * groups,), F32),
         in_specs=[spec(SMEM), spec(SMEM)],
         out_specs=spec(SMEM),
         cost_estimate=pl.CostEstimate(flops=2000000, bytes_accessed=4000000, transcendentals=0),
@@ -421,7 +426,7 @@
         out_shape=[pltpu.VMEM((2, STRIP_ROWS, 256), F32)] * 2,
         in_specs=[spec(SMEM), spec(VMEM)],
         out_specs=[spec(VMEM)] * 2,
-    )(coef, in_vmem(gathered))
+    )(pltpu.with_memory_space_constraint(coef, pltpu.SMEM), in_vmem(gathered))
     route = [(low, low ^ half) for low in range(groups)]
     return mine + lax.ppermute(other, "date", route)
 

time: 62.2 us -> 61 us (0.981)
  Pallas kernels: 17.1 us -> 15.4 us
  local copies, waits for them, and re-layouts: 0.73 us -> 1.39 us
    ppermute x3, waiting for transfers between devices: 8.04 us -> 7.23 us  [per_device(): recvs[which] = lax.ppermute(sends[slot], 'date', route)]
    pallas_call x1, Pallas kernels: 0.95 us -> 0.23 us  [per_device(): pl.pallas_call(sum_kernel, name='sums', out_shape=[pltpu.VMEM((2, STRIP_R...]
    unnamed x7, local copies, waits for them, and re-layouts: 0.02 us -> 0.67 us
  transfers between devices with their start and end apart: 9 -> 9, of which waited for: 6 -> 6; matrix products, arithmetic and copies ran while one was open for 1% -> 1% of each run, Pallas kernels for 15% -> 14%
where the time goes in v4:
time: 61 us; the launch traced here: 60 us
  starting transfers between devices  21.5 us (35%)
  waiting for transfers between devices  21 us (34%)
  Pallas kernels  15.4 us (25%)
  local copies, waits for them, and re-layouts  1.39 us (2%)
  other arithmetic  0.63 us (1%)
    all_to_all x1, starting transfers between devices, per_device(): lax.all_to_all(phases, 'date', 0, 0, tiled=True, axis_index_groups=halves)  9.95 us
    all_to_all x1, waiting for transfers between devices, per_device(): lax.all_to_all(phases, 'date', 0, 0, tiled=True, axis_index_groups=halves)  8.03 us
    ppermute x3, starting transfers between devices, per_device(): recvs[which] = lax.ppermute(sends[slot], 'date', route)  7.27 us
    ppermute x3, waiting for transfers between devices, per_device(): recvs[which] = lax.ppermute(sends[slot], 'date', route)  7.23 us
    pallas_call x2, Pallas kernels, phases_of(): pl.pallas_call(functools.partial(conv_kernel, matchings), out_shape=pltpu...  6.7 us
    ppermute x1, waiting for transfers between devices, per_device(): return mine + lax.ppermute(other, 'date', route)  3.04 us
    pallas_call x1, Pallas kernels, per_device(): pl.pallas_call(coef_kernel, name='coef', out_shape=pltpu.SMEM((12 * group...  2.7 us
    ppermute x1, starting transfers between devices, per_device(): return mine + lax.ppermute(other, 'date', route)  2.28 us
  transfers between devices with their start and end apart: 9, of which 6 were waited for; matrix products, arithmetic and copies ran while one was open for 1% of the time, Pallas kernels for 14%

profile of v4, /device:TPU:2, one launch (start us, length us, event | category | flops | bytes accessed | tf_op | source)
XLA Modules:
  0.0 60.0 jit_solution(6404126337862181794)
XLA Ops:
  0.0 2.1 %prep.1 = (bf16[2,32,2176]{2,1,0:T(8,128)(2,1)S(1)}, bf16[2,32,2176]{2,1,0:T(8,128)(2,1)S(1)}, bf16[2,32,2176]{2,1,0:T(8,128)(2,1)S(1)}) custom-call(s32[2,96]{1,0:T(2,128)} %bitcast.17, bf16[2,2,32,4096]{3,2,1,0:T(8,128)(2,1)} %scenes_ref.3), custom_call_target="tpu_custom_call" | custom-call | tf_op jit(solution)/shard_map/prep/pallas_call | solution.py:332
  2.1 1.9 %collective-permute-start = (bf16[2,32,2176]{2,1,0:T(8,128)(2,1)S(1)}, bf16[2,32,2176]{2,1,0:T(8,128)(2,1)S(1)}, u32[]{:S(2)}, u32[]{:S(2)}) collective-permute-start(bf16[2,32,2176]{2,1,0:T(8,128)(2,1)S(1)} %get-tuple-element.15), channel_id=1, source_target_pairs={{0,4},{4,0},{8,12},{12,8},{16,20},{20,16},{24,28},{28,24},{32,36},... | collective-permute-start | bytes 835592 | tf_op jit(solution)/shard_map/ppermute | solution.py:352
  4.0 3.3 %collective-permute-start.1 = (bf16[2,32,2176]{2,1,0:T(8,128)(2,1)S(1)}, bf16[2,32,2176]{2,1,0:T(8,128)(2,1)S(1)}, u32[]{:S(2)}, u32[]{:S(2)}) collective-permute-start(bf16[2,32,2176]{2,1,0:T(8,128)(2,1)S(1)} %get-tuple-element.16), channel_id=1, source_target_pairs={{0,8},{4,12},{8,0},{12,4},{16,24},{20,28},{24,16},{28,20},{32,40},... | collective-permute-start | bytes 835592 | tf_op jit(solution)/shard_map/ppermute | solution.py:352
  7.2 2.1 %collective-permute-start.4 = (bf16[2,32,2176]{2,1,0:T(8,128)(2,1)S(1)}, bf16[2,32,2176]{2,1,0:T(8,128)(2,1)S(1)}, u32[]{:S(2)}, u32[]{:S(2)}) collective-permute-start(bf16[2,32,2176]{2,1,0:T(8,128)(2,1)S(1)} %get-tuple-element.19), channel_id=1, source_target_pairs={{0,128},{4,132},{8,136},{12,140},{16,144},{20,148},{24,152},{28,15... | collective-permute-start | bytes 835592 | tf_op jit(solution)/shard_map/ppermute | solution.py:352
  9.4 2.1 %own.1 = (bf16[2,32,2176]{2,1,0:T(8,128)(2,1)S(1)}, bf16[2,32,2176]{2,1,0:T(8,128)(2,1)S(1)}, bf16[2,32,2176]{2,1,0:T(8,128)(2,1)S(1)}, f32[3,8,128]{2,1,0:T(8,128)S(1)}) custom-call(s32[2,96]{1,0:T(2,128)} %bitcast.18, bf16[2,2,32,4096]{3,2,1,0:T(8,128)(2,1)} %scenes_ref.3), custom_call_target="tpu_custom_call" | custom-call | tf_op jit(solution)/shard_map/own/pallas_call | solution.py:340
  11.5 0.7 %copy-done.1 = bf16[3,3,64,2]{2,3,1,0:T(2,128)(2,1)S(1)} copy-done((bf16[3,3,64,2]{2,3,1,0:T(2,128)(2,1)S(1)}, bf16[3,3,64,2]{2,3,1,0:T(2,128)(2,1)}, u32[]{:S(2)}) %copy-start.1) | copy-done | bytes 2328
  12.4 4.0 %collective-permute-done.refs_0_ = bf16[2,32,2176]{2,1,0:T(8,128)(2,1)S(1)} collective-permute-done((bf16[2,32,2176]{2,1,0:T(8,128)(2,1)S(1)}, bf16[2,32,2176]{2,1,0:T(8,128)(2,1)S(1)}, u32[]{:S(2)}, u32[]{:S(2)}) %collective-permute-start) | collective-permute-done | bytes 278560 | tf_op jit(solution)/shard_map/ppermute | solution.py:352
  16.4 3.3 %collective-permute-done.1.refs_1_ = bf16[2,32,2176]{2,1,0:T(8,128)(2,1)S(1)} collective-permute-done((bf16[2,32,2176]{2,1,0:T(8,128)(2,1)S(1)}, bf16[2,32,2176]{2,1,0:T(8,128)(2,1)S(1)}, u32[]{:S(2)}, u32[]{:S(2)}) %collective-permute-start.1) | collective-permute-done | bytes 278560 | tf_op jit(solution)/shard_map/ppermute | solution.py:352
  19.6 1.0 %shard_map.64.own_ref = bf16[8,1152]{1,0:T(8,128)(2,1)S(1)} custom-call(f32[3,8,128]{2,1,0:T(8,128)S(1)} %get-tuple-element.14.sign_ref, bf16[2,32,2176]{2,1,0:T(8,128)(2,1)S(1)} %collective-permute-done.refs_0_, bf16[2,32,2176]{2,1,0:T(8,128)(2,1)S(1)} %collective-permute-done.1.refs_1_, bf16[2,32,2176]{2,1,0:T(8,128)(2,1)S(1)} %get-tuple-element.17.refs_2_, ...), custom_call_target="tpu_custom_call" | custom-call | tf_op jit(solution)/shard_map/pallas_call | solution.py:373
  20.7 0.5 collective-permute-start.2
  21.2 0.6 %shard_map.65.own_ref = bf16[8,1152]{1,0:T(8,128)(2,1)S(1)} custom-call(f32[3,8,128]{2,1,0:T(8,128)S(1)} %get-tuple-element.14.sign_ref, bf16[2,32,2176]{2,1,0:T(8,128)(2,1)S(1)} %collective-permute-done.4.refs_0_, bf16[2,32,2176]{2,1,0:T(8,128)(2,1)S(1)} %get-tuple-element.20.refs_1_), custom_call_target="tpu_custom_call" | custom-call | tf_op jit(solution)/shard_map/pallas_call | solution.py:373
  21.9 1.4 %collective-permute-start.6 = (bf16[8,1152]{1,0:T(8,128)(2,1)S(1)}, bf16[8,1152]{1,0:T(8,128)(2,1)S(1)}, u32[]{:S(2)}, u32[]{:S(2)}) collective-permute-start(bf16[8,1152]{1,0:T(8,128)(2,1)S(1)} %shard_map.65.own_ref), channel_id=1, source_target_pairs={{1,0},{2,1},{3,2},{0,3},{5,4},{6,5},{7,6},{4,7},{9,8},{10,9},{11,1... | collective-permute-start | bytes 55304 | tf_op jit(solution)/shard_map/ppermute | solution.py:385
  23.3 0.3 copy.13
  23.5 0.3 reshape.10.w2_ref
  23.8 0.9 %collective-permute-done.6.down_ref = bf16[8,1152]{1,0:T(8,128)(2,1)S(1)} collective-permute-done((bf16[8,1152]{1,0:T(8,128)(2,1)S(1)}, bf16[8,1152]{1,0:T(8,128)(2,1)S(1)}, u32[]{:S(2)}, u32[]{:S(2)}) %collective-permute-start.6) | collective-permute-done | bytes 18464 | tf_op jit(solution)/shard_map/ppermute | solution.py:385
  24.7 1.7 %collective-permute-done.5.up_ref = bf16[8,1152]{1,0:T(8,128)(2,1)S(1)} collective-permute-done((bf16[8,1152]{1,0:T(8,128)(2,1)S(1)}, bf16[8,1152]{1,0:T(8,128)(2,1)S(1)}, u32[]{:S(2)}, u32[]{:S(2)}) %collective-permute-start.5) | collective-permute-done | bytes 18464 | tf_op jit(solution)/shard_map/ppermute | solution.py:384
  26.4 2.2 %shard_map.66.refs_0_ = bf16[1,8,128]{2,1,0:T(8,128)(2,1)S(1)} custom-call(bf16[8,1152]{1,0:T(8,128)(2,1)S(1)} %shard_map.65.own_ref, bf16[8,1152]{1,0:T(8,128)(2,1)S(1)} %collective-permute-done.5.up_ref, bf16[8,1152]{1,0:T(8,128)(2,1)S(1)} %collective-permute-done.6.down_ref, bf16[2,64,72]{2,1,0:T(8,128)(2,1)S(1)} %pad_maximum_fusion.w1_ref, ...), custom_call_target="tpu_custom_call" | custom-call | tf_op jit(solution)/shard_map/pallas_call | solution.py:389
  28.7 4.5 %shard_map.67 = bf16[32,3,8,128]{3,2,1,0:T(8,128)(2,1)} custom-call(bf16[8,1152]{1,0:T(8,128)(2,1)S(1)} %shard_map.64.own_ref, bf16[8,1152]{1,0:T(8,128)(2,1)S(1)} %collective-permute-done.2.up_ref, bf16[8,1152]{1,0:T(8,128)(2,1)S(1)} %collective-permute-done.3.down_ref, bf16[2,64,72]{2,1,0:T(8,128)(2,1)S(1)} %pad_maximum_fusion.w1_ref, ...), custom_call_target="tpu_custom_call" | custom-call | tf_op jit(solution)/shard_map/pallas_call | solution.py:389
  33.2 9.9 %all-to-all-start = ((bf16[32,3,8,128]{3,2,1,0:T(8,128)(2,1)}), bf16[32,3,8,128]{3,2,1,0:T(8,128)(2,1)S(1)}, u32[]{:S(2)}, u32[]{:S(2)}) async-start(bf16[32,3,8,128]{3,2,1,0:T(8,128)(2,1)} %shard_map.67), calls=%async_computation | async-start | bytes 393216 | tf_op jit(solution)/shard_map/all_to_all | solution.py:421
  43.1 2.7 %coef.1.coef_ref = f32[768]{0:T(1024)S(4)} custom-call(s32[2,96]{1,0:T(2,128)} %bitcast.19, f32[96,128]{1,0:T(8,128)} %bitcast.16), custom_call_target="tpu_custom_call" | custom-call | flops 2000000 | bytes 4000000 | tf_op jit(solution)/shard_map/coef/pallas_call | solution.py:354
  45.8 8.0 %all-to-all-done.gathered_ref = bf16[32,3,8,128]{3,2,1,0:T(8,128)(2,1)S(1)} async-done(((bf16[32,3,8,128]{3,2,1,0:T(8,128)(2,1)}), bf16[32,3,8,128]{3,2,1,0:T(8,128)(2,1)S(1)}, u32[]{:S(2)}, u32[]{:S(2)}) %all-to-all-start) | async-done | bytes 196640 | tf_op jit(solution)/shard_map/all_to_all | solution.py:421
  54.1 2.3 %collective-permute-start.7 = (f32[2,8,256]{2,1,0:T(8,128)S(1)}, f32[2,8,256]{2,1,0:T(8,128)S(1)}, u32[]{:S(2)}, u32[]{:S(2)}) collective-permute-start(f32[2,8,256]{2,1,0:T(8,128)S(1)} %get-tuple-element.22), channel_id=1, source_target_pairs={{0,128},{4,132},{8,136},{12,140},{16,144},{20,148},{24,152},{28,15... | collective-permute-start | bytes 49160 | tf_op jit(solution)/shard_map/ppermute | solution.py:431
  56.4 3.0 %collective-permute-done.7 = f32[2,8,256]{2,1,0:T(8,128)S(1)} collective-permute-done((f32[2,8,256]{2,1,0:T(8,128)S(1)}, f32[2,8,256]{2,1,0:T(8,128)S(1)}, u32[]{:S(2)}, u32[]{:S(2)}) %collective-permute-start.7) | collective-permute-done | bytes 16416 | tf_op jit(solution)/shard_map/ppermute | solution.py:431
  59.4 0.6 %add.9 = f32[2,8,256]{2,1,0:T(8,128)} add(f32[2,8,256]{2,1,0:T(8,128)S(1)} %get-tuple-element.21, f32[2,8,256]{2,1,0:T(8,128)S(1)} %collective-permute-done.7) | non-fusion elementwise | flops 4096 | bytes 49152 | tf_op jit(solution)/shard_map/add | solution.py:431
  (17 shorter events, 0.6 us)
Async XLA Ops:
  2.1 14.3 %collective-permute-start = (bf16[2,32,2176]{2,1,0:T(8,128)(2,1)S(1)}, bf16[2,32,2176]{2,1,0:T(8,128)(2,1)S(1)}, u32[]{:S(2)}, u32[]{:S(2)}) collective-permute-start(bf16[2,32,2176]{2,1,0:T(8,128)(2,1)S(1)} %get-tuple-element.15), channel_id=1, source_target_pairs={{0,4},{4,0},{8,12},{12,8},{16,20},{20,16},{24,28},{28,24},{32,36},... | collective-permute-start | bytes 835592 | tf_op jit(solution)/shard_map/ppermute | solution.py:352
  4.0 15.7 %collective-permute-start.1 = (bf16[2,32,2176]{2,1,0:T(8,128)(2,1)S(1)}, bf16[2,32,2176]{2,1,0:T(8,128)(2,1)S(1)}, u32[]{:S(2)}, u32[]{:S(2)}) collective-permute-start(bf16[2,32,2176]{2,1,0:T(8,128)(2,1)S(1)} %get-tuple-element.16), channel_id=1, source_target_pairs={{0,8},{4,12},{8,0},{12,4},{16,24},{20,28},{24,16},{28,20},{32,40},... | collective-permute-start | bytes 835592 | tf_op jit(solution)/shard_map/ppermute | solution.py:352
  7.2 14.0 %collective-permute-start.4 = (bf16[2,32,2176]{2,1,0:T(8,128)(2,1)S(1)}, bf16[2,32,2176]{2,1,0:T(8,128)(2,1)S(1)}, u32[]{:S(2)}, u32[]{:S(2)}) collective-permute-start(bf16[2,32,2176]{2,1,0:T(8,128)(2,1)S(1)} %get-tuple-element.19), channel_id=1, source_target_pairs={{0,128},{4,132},{8,136},{12,140},{16,144},{20,148},{24,152},{28,15... | collective-permute-start | bytes 835592 | tf_op jit(solution)/shard_map/ppermute | solution.py:352
  9.4 2.1 %copy-start.2 = (bf16[3,3,1,64]{3,1,2,0:T(4,128)(2,1)S(1)}, bf16[3,3,1,64]{3,1,2,0:T(4,128)(2,1)}, u32[]{:S(2)}) copy-start(bf16[3,3,1,64]{3,1,2,0:T(4,128)(2,1)} %param.10) | copy-start | bytes 3460
  11.5 0.7 %copy-start.1 = (bf16[3,3,64,2]{2,3,1,0:T(2,128)(2,1)S(1)}, bf16[3,3,64,2]{2,3,1,0:T(2,128)(2,1)}, u32[]{:S(2)}) copy-start(bf16[3,3,64,2]{2,3,1,0:T(2,128)(2,1)} %param.8) | copy-start | bytes 6916
  20.6 8.0 %collective-permute-start.3 = (bf16[8,1152]{1,0:T(8,128)(2,1)S(1)}, bf16[8,1152]{1,0:T(8,128)(2,1)S(1)}, u32[]{:S(2)}, u32[]{:S(2)}) collective-permute-start(bf16[8,1152]{1,0:T(8,128)(2,1)S(1)} %shard_map.64.own_ref), channel_id=1, source_target_pairs={{1,0},{2,1},{3,2},{0,3},{5,4},{6,5},{7,6},{4,7},{9,8},{10,9},{11,1... | collective-permute-start | bytes 55304 | tf_op jit(solution)/shard_map/ppermute | solution.py:385
  20.7 8.0 %collective-permute-start.2 = (bf16[8,1152]{1,0:T(8,128)(2,1)S(1)}, bf16[8,1152]{1,0:T(8,128)(2,1)S(1)}, u32[]{:S(2)}, u32[]{:S(2)}) collective-permute-start(bf16[8,1152]{1,0:T(8,128)(2,1)S(1)} %shard_map.64.own_ref), channel_id=1, source_target_pairs={{0,1},{1,2},{2,3},{3,0},{4,5},{5,6},{6,7},{7,4},{8,9},{9,10},{10,1... | collective-permute-start | bytes 55304 | tf_op jit(solution)/shard_map/ppermute | solution.py:384
  21.2 2.1 %copy-start = (bf16[2,3,3,64,64]{4,3,2,1,0:T(8,128)(2,1)S(1)}, bf16[2,3,3,64,64]{4,3,2,1,0:T(8,128)(2,1)}, u32[]{:S(2)}) copy-start(bf16[2,3,3,64,64]{4,3,2,1,0:T(8,128)(2,1)} %param.9) | copy-start | bytes 442372
  21.9 2.9 %collective-permute-start.6 = (bf16[8,1152]{1,0:T(8,128)(2,1)S(1)}, bf16[8,1152]{1,0:T(8,128)(2,1)S(1)}, u32[]{:S(2)}, u32[]{:S(2)}) collective-permute-start(bf16[8,1152]{1,0:T(8,128)(2,1)S(1)} %shard_map.65.own_ref), channel_id=1, source_target_pairs={{1,0},{2,1},{3,2},{0,3},{5,4},{6,5},{7,6},{4,7},{9,8},{10,9},{11,1... | collective-permute-start | bytes 55304 | tf_op jit(solution)/shard_map/ppermute | solution.py:385
  23.3 3.2 %collective-permute-start.5 = (bf16[8,1152]{1,0:T(8,128)(2,1)S(1)}, bf16[8,1152]{1,0:T(8,128)(2,1)S(1)}, u32[]{:S(2)}, u32[]{:S(2)}) collective-permute-start(bf16[8,1152]{1,0:T(8,128)(2,1)S(1)} %shard_map.65.own_ref), channel_id=1, source_target_pairs={{0,1},{1,2},{2,3},{3,0},{4,5},{5,6},{6,7},{7,4},{8,9},{9,10},{10,1... | collective-permute-start | bytes 55304 | tf_op jit(solution)/shard_map/ppermute | solution.py:384
  33.2 20.7 %all-to-all-start = ((bf16[32,3,8,128]{3,2,1,0:T(8,128)(2,1)}), bf16[32,3,8,128]{3,2,1,0:T(8,128)(2,1)S(1)}, u32[]{:S(2)}, u32[]{:S(2)}) async-start(bf16[32,3,8,128]{3,2,1,0:T(8,128)(2,1)} %shard_map.67), calls=%async_computation | async-start | bytes 393216 | tf_op jit(solution)/shard_map/all_to_all | solution.py:421
  54.1 5.3 %collective-permute-start.7 = (f32[2,8,256]{2,1,0:T(8,128)S(1)}, f32[2,8,256]{2,1,0:T(8,128)S(1)}, u32[]{:S(2)}, u32[]{:S(2)}) collective-permute-start(f32[2,8,256]{2,1,0:T(8,128)S(1)} %get-tuple-element.22), channel_id=1, source_target_pairs={{0,128},{4,132},{8,136},{12,140},{16,144},{20,148},{24,152},{28,15... | collective-permute-start | bytes 49160 | tf_op jit(solution)/shard_map/ppermute | solution.py:431

commit v5 on v4

--- a/solution.py
+++ b/solution.py
@@ -205,8 +205,14 @@
                 if q != 1:
                     value = pltpu.roll(value, 1 if q == 0 else PART - 1, 1)
                 taps[k : k + 8, base : base + PART] = value.astype(BF)
-    hidden_a[...] = jnp.zeros_like(hidden_a)
-    hidden_b[...] = jnp.zeros_like(hidden_b)
+    for hidden, written in (
+        (hidden_a, ((128, 1152), (0, 1024))),
+        (hidden_b, ((128, 1024), (128, 1024))),
+    ):
+        for part, (lo, hi) in enumerate(written):
+            for start in (guard + lo - 128, guard + hi):
+                side = hidden.shape[0], hidden.shape[2], 128
+                hidden[:, part, :, start : start + 128] = jnp.zeros(side, BF)
 
     def masked(value, part, lo, hi):
         lo, hi = part * PART + lo, part * PART + hi

time: 61 us -> 60.9 us (level)
  no operation moved by 1% of the time
where the time goes in v5:
time: 60.9 us; the launch traced here: 60 us
  starting transfers between devices  21.5 us (35%)
  waiting for transfers between devices  21 us (34%)
  Pallas kernels  15.4 us (25%)
  local copies, waits for them, and re-layouts  1.39 us (2%)
  other arithmetic  0.63 us (1%)
    all_to_all x1, starting transfers between devices, per_device(): lax.all_to_all(phases, 'date', 0, 0, tiled=True, axis_index_groups=halves)  9.95 us
    all_to_all x1, waiting for transfers between devices, per_device(): lax.all_to_all(phases, 'date', 0, 0, tiled=True, axis_index_groups=halves)  8.03 us
    ppermute x3, starting transfers between devices, per_device(): recvs[which] = lax.ppermute(sends[slot], 'date', route)  7.27 us
    ppermute x3, waiting for transfers between devices, per_device(): recvs[which] = lax.ppermute(sends[slot], 'date', route)  7.23 us
    pallas_call x2, Pallas kernels, phases_of(): pl.pallas_call(functools.partial(conv_kernel, matchings), out_shape=pltpu...  6.67 us
    ppermute x1, waiting for transfers between devices, per_device(): return mine + lax.ppermute(other, 'date', route)  3.05 us
    pallas_call x1, Pallas kernels, per_device(): pl.pallas_call(coef_kernel, name='coef', out_shape=pltpu.SMEM((12 * group...  2.7 us
    ppermute x1, starting transfers between devices, per_device(): return mine + lax.ppermute(other, 'date', route)  2.27 us
  transfers between devices with their start and end apart: 9, of which 6 were waited for; matrix products, arithmetic and copies ran while one was open for 1% of the time, Pallas kernels for 14%

profile of v5, /device:TPU:2, one launch (start us, length us, event | category | flops | bytes accessed | tf_op | source)
XLA Modules:
  0.0 60.0 jit_solution(228518914004246868)
XLA Ops:
  0.0 2.1 %prep.1 = (bf16[2,32,2176]{2,1,0:T(8,128)(2,1)S(1)}, bf16[2,32,2176]{2,1,0:T(8,128)(2,1)S(1)}, bf16[2,32,2176]{2,1,0:T(8,128)(2,1)S(1)}) custom-call(s32[2,96]{1,0:T(2,128)} %bitcast.17, bf16[2,2,32,4096]{3,2,1,0:T(8,128)(2,1)} %scenes_ref.3), custom_call_target="tpu_custom_call" | custom-call | tf_op jit(solution)/shard_map/prep/pallas_call | solution.py:338
  2.1 1.9 %collective-permute-start = (bf16[2,32,2176]{2,1,0:T(8,128)(2,1)S(1)}, bf16[2,32,2176]{2,1,0:T(8,128)(2,1)S(1)}, u32[]{:S(2)}, u32[]{:S(2)}) collective-permute-start(bf16[2,32,2176]{2,1,0:T(8,128)(2,1)S(1)} %get-tuple-element.15), channel_id=1, source_target_pairs={{0,4},{4,0},{8,12},{12,8},{16,20},{20,16},{24,28},{28,24},{32,36},... | collective-permute-start | bytes 835592 | tf_op jit(solution)/shard_map/ppermute | solution.py:358
  4.0 3.3 %collective-permute-start.1 = (bf16[2,32,2176]{2,1,0:T(8,128)(2,1)S(1)}, bf16[2,32,2176]{2,1,0:T(8,128)(2,1)S(1)}, u32[]{:S(2)}, u32[]{:S(2)}) collective-permute-start(bf16[2,32,2176]{2,1,0:T(8,128)(2,1)S(1)} %get-tuple-element.16), channel_id=1, source_target_pairs={{0,8},{4,12},{8,0},{12,4},{16,24},{20,28},{24,16},{28,20},{32,40},... | collective-permute-start | bytes 835592 | tf_op jit(solution)/shard_map/ppermute | solution.py:358
  7.2 2.1 %collective-permute-start.4 = (bf16[2,32,2176]{2,1,0:T(8,128)(2,1)S(1)}, bf16[2,32,2176]{2,1,0:T(8,128)(2,1)S(1)}, u32[]{:S(2)}, u32[]{:S(2)}) collective-permute-start(bf16[2,32,2176]{2,1,0:T(8,128)(2,1)S(1)} %get-tuple-element.19), channel_id=1, source_target_pairs={{0,128},{4,132},{8,136},{12,140},{16,144},{20,148},{24,152},{28,15... | collective-permute-start | bytes 835592 | tf_op jit(solution)/shard_map/ppermute | solution.py:358
  9.4 2.1 %own.1 = (bf16[2,32,2176]{2,1,0:T(8,128)(2,1)S(1)}, bf16[2,32,2176]{2,1,0:T(8,128)(2,1)S(1)}, bf16[2,32,2176]{2,1,0:T(8,128)(2,1)S(1)}, f32[3,8,128]{2,1,0:T(8,128)S(1)}) custom-call(s32[2,96]{1,0:T(2,128)} %bitcast.18, bf16[2,2,32,4096]{3,2,1,0:T(8,128)(2,1)} %scenes_ref.3), custom_call_target="tpu_custom_call" | custom-call | tf_op jit(solution)/shard_map/own/pallas_call | solution.py:346
  11.5 0.7 %copy-done.1 = bf16[3,3,64,2]{2,3,1,0:T(2,128)(2,1)S(1)} copy-done((bf16[3,3,64,2]{2,3,1,0:T(2,128)(2,1)S(1)}, bf16[3,3,64,2]{2,3,1,0:T(2,128)(2,1)}, u32[]{:S(2)}) %copy-start.1) | copy-done | bytes 2328
  12.4 4.0 %collective-permute-done.refs_0_ = bf16[2,32,2176]{2,1,0:T(8,128)(2,1)S(1)} collective-permute-done((bf16[2,32,2176]{2,1,0:T(8,128)(2,1)S(1)}, bf16[2,32,2176]{2,1,0:T(8,128)(2,1)S(1)}, u32[]{:S(2)}, u32[]{:S(2)}) %collective-permute-start) | collective-permute-done | bytes 278560 | tf_op jit(solution)/shard_map/ppermute | solution.py:358
  16.4 3.3 %collective-permute-done.1.refs_1_ = bf16[2,32,2176]{2,1,0:T(8,128)(2,1)S(1)} collective-permute-done((bf16[2,32,2176]{2,1,0:T(8,128)(2,1)S(1)}, bf16[2,32,2176]{2,1,0:T(8,128)(2,1)S(1)}, u32[]{:S(2)}, u32[]{:S(2)}) %collective-permute-start.1) | collective-permute-done | bytes 278560 | tf_op jit(solution)/shard_map/ppermute | solution.py:358
  19.6 1.0 %shard_map.64.own_ref = bf16[8,1152]{1,0:T(8,128)(2,1)S(1)} custom-call(f32[3,8,128]{2,1,0:T(8,128)S(1)} %get-tuple-element.14.sign_ref, bf16[2,32,2176]{2,1,0:T(8,128)(2,1)S(1)} %collective-permute-done.refs_0_, bf16[2,32,2176]{2,1,0:T(8,128)(2,1)S(1)} %collective-permute-done.1.refs_1_, bf16[2,32,2176]{2,1,0:T(8,128)(2,1)S(1)} %get-tuple-element.17.refs_2_, ...), custom_call_target="tpu_custom_call" | custom-call | tf_op jit(solution)/shard_map/pallas_call | solution.py:379
  20.7 0.5 collective-permute-start.2
  21.2 0.6 %shard_map.65.own_ref = bf16[8,1152]{1,0:T(8,128)(2,1)S(1)} custom-call(f32[3,8,128]{2,1,0:T(8,128)S(1)} %get-tuple-element.14.sign_ref, bf16[2,32,2176]{2,1,0:T(8,128)(2,1)S(1)} %collective-permute-done.4.refs_0_, bf16[2,32,2176]{2,1,0:T(8,128)(2,1)S(1)} %get-tuple-element.20.refs_1_), custom_call_target="tpu_custom_call" | custom-call | tf_op jit(solution)/shard_map/pallas_call | solution.py:379
  21.9 1.4 %collective-permute-start.6 = (bf16[8,1152]{1,0:T(8,128)(2,1)S(1)}, bf16[8,1152]{1,0:T(8,128)(2,1)S(1)}, u32[]{:S(2)}, u32[]{:S(2)}) collective-permute-start(bf16[8,1152]{1,0:T(8,128)(2,1)S(1)} %shard_map.65.own_ref), channel_id=1, source_target_pairs={{1,0},{2,1},{3,2},{0,3},{5,4},{6,5},{7,6},{4,7},{9,8},{10,9},{11,1... | collective-permute-start | bytes 55304 | tf_op jit(solution)/shard_map/ppermute | solution.py:391
  23.3 0.3 copy.13
  23.5 0.3 reshape.10.w2_ref
  23.8 0.9 %collective-permute-done.6.down_ref = bf16[8,1152]{1,0:T(8,128)(2,1)S(1)} collective-permute-done((bf16[8,1152]{1,0:T(8,128)(2,1)S(1)}, bf16[8,1152]{1,0:T(8,128)(2,1)S(1)}, u32[]{:S(2)}, u32[]{:S(2)}) %collective-permute-start.6) | collective-permute-done | bytes 18464 | tf_op jit(solution)/shard_map/ppermute | solution.py:391
  24.7 1.7 %collective-permute-done.5.up_ref = bf16[8,1152]{1,0:T(8,128)(2,1)S(1)} collective-permute-done((bf16[8,1152]{1,0:T(8,128)(2,1)S(1)}, bf16[8,1152]{1,0:T(8,128)(2,1)S(1)}, u32[]{:S(2)}, u32[]{:S(2)}) %collective-permute-start.5) | collective-permute-done | bytes 18464 | tf_op jit(solution)/shard_map/ppermute | solution.py:390
  26.4 2.2 %shard_map.66.refs_0_ = bf16[1,8,128]{2,1,0:T(8,128)(2,1)S(1)} custom-call(bf16[8,1152]{1,0:T(8,128)(2,1)S(1)} %shard_map.65.own_ref, bf16[8,1152]{1,0:T(8,128)(2,1)S(1)} %collective-permute-done.5.up_ref, bf16[8,1152]{1,0:T(8,128)(2,1)S(1)} %collective-permute-done.6.down_ref, bf16[2,64,72]{2,1,0:T(8,128)(2,1)S(1)} %pad_maximum_fusion.w1_ref, ...), custom_call_target="tpu_custom_call" | custom-call | tf_op jit(solution)/shard_map/pallas_call | solution.py:395
  28.7 4.5 %shard_map.67 = bf16[32,3,8,128]{3,2,1,0:T(8,128)(2,1)} custom-call(bf16[8,1152]{1,0:T(8,128)(2,1)S(1)} %shard_map.64.own_ref, bf16[8,1152]{1,0:T(8,128)(2,1)S(1)} %collective-permute-done.2.up_ref, bf16[8,1152]{1,0:T(8,128)(2,1)S(1)} %collective-permute-done.3.down_ref, bf16[2,64,72]{2,1,0:T(8,128)(2,1)S(1)} %pad_maximum_fusion.w1_ref, ...), custom_call_target="tpu_custom_call" | custom-call | tf_op jit(solution)/shard_map/pallas_call | solution.py:395
  33.1 9.9 %all-to-all-start = ((bf16[32,3,8,128]{3,2,1,0:T(8,128)(2,1)}), bf16[32,3,8,128]{3,2,1,0:T(8,128)(2,1)S(1)}, u32[]{:S(2)}, u32[]{:S(2)}) async-start(bf16[32,3,8,128]{3,2,1,0:T(8,128)(2,1)} %shard_map.67), calls=%async_computation | async-start | bytes 393216 | tf_op jit(solution)/shard_map/all_to_all | solution.py:427
  43.1 2.7 %coef.1.coef_ref = f32[768]{0:T(1024)S(4)} custom-call(s32[2,96]{1,0:T(2,128)} %bitcast.19, f32[96,128]{1,0:T(8,128)} %bitcast.16), custom_call_target="tpu_custom_call" | custom-call | flops 2000000 | bytes 4000000 | tf_op jit(solution)/shard_map/coef/pallas_call | solution.py:360
  45.8 8.0 %all-to-all-done.gathered_ref = bf16[32,3,8,128]{3,2,1,0:T(8,128)(2,1)S(1)} async-done(((bf16[32,3,8,128]{3,2,1,0:T(8,128)(2,1)}), bf16[32,3,8,128]{3,2,1,0:T(8,128)(2,1)S(1)}, u32[]{:S(2)}, u32[]{:S(2)}) %all-to-all-start) | async-done | bytes 196640 | tf_op jit(solution)/shard_map/all_to_all | solution.py:427
  54.1 2.3 %collective-permute-start.7 = (f32[2,8,256]{2,1,0:T(8,128)S(1)}, f32[2,8,256]{2,1,0:T(8,128)S(1)}, u32[]{:S(2)}, u32[]{:S(2)}) collective-permute-start(f32[2,8,256]{2,1,0:T(8,128)S(1)} %get-tuple-element.22), channel_id=1, source_target_pairs={{0,128},{4,132},{8,136},{12,140},{16,144},{20,148},{24,152},{28,15... | collective-permute-start | bytes 49160 | tf_op jit(solution)/shard_map/ppermute | solution.py:437
  56.3 3.0 %collective-permute-done.7 = f32[2,8,256]{2,1,0:T(8,128)S(1)} collective-permute-done((f32[2,8,256]{2,1,0:T(8,128)S(1)}, f32[2,8,256]{2,1,0:T(8,128)S(1)}, u32[]{:S(2)}, u32[]{:S(2)}) %collective-permute-start.7) | collective-permute-done | bytes 16416 | tf_op jit(solution)/shard_map/ppermute | solution.py:437
  59.4 0.6 %add.9 = f32[2,8,256]{2,1,0:T(8,128)} add(f32[2,8,256]{2,1,0:T(8,128)S(1)} %get-tuple-element.21, f32[2,8,256]{2,1,0:T(8,128)S(1)} %collective-permute-done.7) | non-fusion elementwise | flops 4096 | bytes 49152 | tf_op jit(solution)/shard_map/add | solution.py:437
  (17 shorter events, 0.6 us)
Async XLA Ops:
  2.1 14.3 %collective-permute-start = (bf16[2,32,2176]{2,1,0:T(8,128)(2,1)S(1)}, bf16[2,32,2176]{2,1,0:T(8,128)(2,1)S(1)}, u32[]{:S(2)}, u32[]{:S(2)}) collective-permute-start(bf16[2,32,2176]{2,1,0:T(8,128)(2,1)S(1)} %get-tuple-element.15), channel_id=1, source_target_pairs={{0,4},{4,0},{8,12},{12,8},{16,20},{20,16},{24,28},{28,24},{32,36},... | collective-permute-start | bytes 835592 | tf_op jit(solution)/shard_map/ppermute | solution.py:358
  4.0 15.7 %collective-permute-start.1 = (bf16[2,32,2176]{2,1,0:T(8,128)(2,1)S(1)}, bf16[2,32,2176]{2,1,0:T(8,128)(2,1)S(1)}, u32[]{:S(2)}, u32[]{:S(2)}) collective-permute-start(bf16[2,32,2176]{2,1,0:T(8,128)(2,1)S(1)} %get-tuple-element.16), channel_id=1, source_target_pairs={{0,8},{4,12},{8,0},{12,4},{16,24},{20,28},{24,16},{28,20},{32,40},... | collective-permute-start | bytes 835592 | tf_op jit(solution)/shard_map/ppermute | solution.py:358
  7.2 14.0 %collective-permute-start.4 = (bf16[2,32,2176]{2,1,0:T(8,128)(2,1)S(1)}, bf16[2,32,2176]{2,1,0:T(8,128)(2,1)S(1)}, u32[]{:S(2)}, u32[]{:S(2)}) collective-permute-start(bf16[2,32,2176]{2,1,0:T(8,128)(2,1)S(1)} %get-tuple-element.19), channel_id=1, source_target_pairs={{0,128},{4,132},{8,136},{12,140},{16,144},{20,148},{24,152},{28,15... | collective-permute-start | bytes 835592 | tf_op jit(solution)/shard_map/ppermute | solution.py:358
  9.4 2.1 %copy-start.2 = (bf16[3,3,1,64]{3,1,2,0:T(4,128)(2,1)S(1)}, bf16[3,3,1,64]{3,1,2,0:T(4,128)(2,1)}, u32[]{:S(2)}) copy-start(bf16[3,3,1,64]{3,1,2,0:T(4,128)(2,1)} %param.10) | copy-start | bytes 3460
  11.5 0.7 %copy-start.1 = (bf16[3,3,64,2]{2,3,1,0:T(2,128)(2,1)S(1)}, bf16[3,3,64,2]{2,3,1,0:T(2,128)(2,1)}, u32[]{:S(2)}) copy-start(bf16[3,3,64,2]{2,3,1,0:T(2,128)(2,1)} %param.8) | copy-start | bytes 6916
  20.6 8.0 %collective-permute-start.3 = (bf16[8,1152]{1,0:T(8,128)(2,1)S(1)}, bf16[8,1152]{1,0:T(8,128)(2,1)S(1)}, u32[]{:S(2)}, u32[]{:S(2)}) collective-permute-start(bf16[8,1152]{1,0:T(8,128)(2,1)S(1)} %shard_map.64.own_ref), channel_id=1, source_target_pairs={{1,0},{2,1},{3,2},{0,3},{5,4},{6,5},{7,6},{4,7},{9,8},{10,9},{11,1... | collective-permute-start | bytes 55304 | tf_op jit(solution)/shard_map/ppermute | solution.py:391
  20.7 8.0 %collective-permute-start.2 = (bf16[8,1152]{1,0:T(8,128)(2,1)S(1)}, bf16[8,1152]{1,0:T(8,128)(2,1)S(1)}, u32[]{:S(2)}, u32[]{:S(2)}) collective-permute-start(bf16[8,1152]{1,0:T(8,128)(2,1)S(1)} %shard_map.64.own_ref), channel_id=1, source_target_pairs={{0,1},{1,2},{2,3},{3,0},{4,5},{5,6},{6,7},{7,4},{8,9},{9,10},{10,1... | collective-permute-start | bytes 55304 | tf_op jit(solution)/shard_map/ppermute | solution.py:390
  21.2 2.1 %copy-start = (bf16[2,3,3,64,64]{4,3,2,1,0:T(8,128)(2,1)S(1)}, bf16[2,3,3,64,64]{4,3,2,1,0:T(8,128)(2,1)}, u32[]{:S(2)}) copy-start(bf16[2,3,3,64,64]{4,3,2,1,0:T(8,128)(2,1)} %param.9) | copy-start | bytes 442372
  21.9 2.9 %collective-permute-start.6 = (bf16[8,1152]{1,0:T(8,128)(2,1)S(1)}, bf16[8,1152]{1,0:T(8,128)(2,1)S(1)}, u32[]{:S(2)}, u32[]{:S(2)}) collective-permute-start(bf16[8,1152]{1,0:T(8,128)(2,1)S(1)} %shard_map.65.own_ref), channel_id=1, source_target_pairs={{1,0},{2,1},{3,2},{0,3},{5,4},{6,5},{7,6},{4,7},{9,8},{10,9},{11,1... | collective-permute-start | bytes 55304 | tf_op jit(solution)/shard_map/ppermute | solution.py:391
  23.3 3.2 %collective-permute-start.5 = (bf16[8,1152]{1,0:T(8,128)(2,1)S(1)}, bf16[8,1152]{1,0:T(8,128)(2,1)S(1)}, u32[]{:S(2)}, u32[]{:S(2)}) collective-permute-start(bf16[8,1152]{1,0:T(8,128)(2,1)S(1)} %shard_map.65.own_ref), channel_id=1, source_target_pairs={{0,1},{1,2},{2,3},{3,0},{4,5},{5,6},{6,7},{7,4},{8,9},{9,10},{10,1... | collective-permute-start | bytes 55304 | tf_op jit(solution)/shard_map/ppermute | solution.py:390
  33.1 20.7 %all-to-all-start = ((bf16[32,3,8,128]{3,2,1,0:T(8,128)(2,1)}), bf16[32,3,8,128]{3,2,1,0:T(8,128)(2,1)S(1)}, u32[]{:S(2)}, u32[]{:S(2)}) async-start(bf16[32,3,8,128]{3,2,1,0:T(8,128)(2,1)} %shard_map.67), calls=%async_computation | async-start | bytes 393216 | tf_op jit(solution)/shard_map/all_to_all | solution.py:427
  54.1 5.3 %collective-permute-start.7 = (f32[2,8,256]{2,1,0:T(8,128)S(1)}, f32[2,8,256]{2,1,0:T(8,128)S(1)}, u32[]{:S(2)}, u32[]{:S(2)}) collective-permute-start(f32[2,8,256]{2,1,0:T(8,128)S(1)} %get-tuple-element.22), channel_id=1, source_target_pairs={{0,128},{4,132},{8,136},{12,140},{16,144},{20,148},{24,152},{28,15... | collective-permute-start | bytes 49160 | tf_op jit(solution)/shard_map/ppermute | solution.py:437
